TPU v7x, 256 devices: a whole 4x4x8 slice. The times are simulated.
256 devices in a mesh: frag: 64 (over z, y, core), tile: 4 (over x).
Axes of the slice: x: 4, y: 4, z: 8, core: 2. Of those that a mesh axis runs over, the one named last changes fastest.
Arguments:
- core_fock: float32 [512, 256, 256], P('frag', 'tile'), as said below
- intersection: float32 [512, 256, 256], P('frag', 'tile'), as said below
- gamma_tile: float32 [512, 256, 256], P('frag', 'tile'), may hold values from -0.375 to 0.375
- charge_old: float32 [512, 256], P('frag'), may hold values from -6 to 6
- embed_old: float32 [512, 256], P('frag'), may hold values from -4 to 4
- core_pop: float32 [512, 256], P('frag'), may hold values from 0 to 1
- centres: float32 [512, 3, 256], P('frag'), may hold values from -10 to 10
- frag_sizes: int32 [512], P('frag'), may hold values from 20 to 256, as said below
- near_list: int32 [512, 8], P('frag'), may hold values from 0 to 511, as said below
- far_list: int32 [512, 8], P('frag'), may hold values from 0 to 511
Outputs:
- density: float32 [512, 256, 256], P('frag', 'tile')
- esp_matrix: float32 [512, 256, 256], P('frag', 'tile')
Inputs may be any that keep to these rules, and one draw needn't show every extreme that they name: `frag_sizes`: each fragment uses at least 20 basis functions; some fragment uses exactly 256. near_list[f, k] is a fragment whose index differs from f by 1 to 8; the distance 8 occurs. `core_fock`: symmetric in its last two dimensions. `intersection`: symmetric in its last two dimensions.
All inputs are finite; a program needn't handle non-finite values.
Results may differ from a plain program's by a relative error of at most 0.0003.
Values sent between devices are 32-bit elements; how exact they have to be, the bound alone decides.
A program may use at most 64 MiB of HBM per device.

v0:
```python
import jax
import jax.numpy as jnp
from jax import lax
from jax.sharding import PartitionSpec as P

PC = 8
ITERS = 12


precise = lax.Precision.HIGHEST
screening = 0.25


def extended(x, sides, width):
    for axis, dim in sides:
        peers, length = (lax.axis_size(axis), x.shape[dim])
        up = [(i, (i + 1) % peers) for i in range(peers - 1)]
        down = [(j, i) for i, j in up]
        last = lax.slice_in_dim(x, length - width, length, axis=dim)
        leading = lax.slice_in_dim(x, 0, width, axis=dim)
        before = lax.ppermute(last, axis, up)
        after = lax.ppermute(leading, axis, down)
        x = jnp.concatenate([before, x, after], axis=dim)
    return x


def coulomb(centre_set, source):
    dist_sq = (centre_set[0][:, None] - source[1][None, :]) ** 2
    dist_sq = dist_sq + (centre_set[1][:, None] - source[2][None, :]) ** 2
    dist_sq = dist_sq + (centre_set[2][:, None] - source[3][None, :]) ** 2
    return jnp.sum(source[0][None, :] * lax.rsqrt(dist_sq + 1.0), axis=1)


def point_blocks(charges, centres):
    frag_count = charges.shape[0]
    group = charges.shape[1] // PC
    block_charge = jnp.sum(charges.reshape(frag_count, PC, group), axis=2)
    block_place = jnp.mean(centres.reshape(frag_count, 3, PC, group), axis=3)
    return jnp.concatenate([block_charge[:, None, :], block_place], axis=1)


def potentials(centres, near_rows, far_rows, table, blocks):
    basis_count = centres.shape[2]

    def potential_of(inputs):
        centre_set, near_ids, far_ids = inputs

        def add_near(summed, neighbour):
            return (summed + coulomb(centre_set, table[neighbour]), None)

        summed, unused = lax.scan(add_near, jnp.zeros((basis_count,), jnp.float32), near_ids)
        far_source = jnp.transpose(blocks[far_ids], (1, 0, 2)).reshape(4, -1)
        return screening * (summed + coulomb(centre_set, far_source))

    return lax.map(potential_of, (centres, near_rows, far_rows))


def cube_step(sign_est, full_rows):
    squared = jnp.einsum("fij,fjk->fik", sign_est, full_rows, precision=precise)
    return 1.5 * sign_est - 0.5 * jnp.einsum("fij,fjk->fik", squared, full_rows, precision=precise)


def whole_density(fock_matrix, sizes_share, column_index):
    basis_count = fock_matrix.shape[2]
    active = (column_index[None, :] < sizes_share[:, None]).astype(jnp.float32)
    masked = fock_matrix * active[:, :, None] * active[:, None, :]
    frob_norm = jnp.sqrt(jnp.sum(masked * masked, axis=(1, 2)) + 1e-06)
    identity = jnp.eye(basis_count, dtype=jnp.float32)
    start_est = masked / frob_norm[:, None, None] + identity[None] * (1.0 - active)[:, :, None]

    def sweep(sweep_index, sign_est):
        return cube_step(sign_est, sign_est)

    sign_est = lax.fori_loop(0, ITERS, sweep, start_est)
    return 0.5 * (identity[None] - sign_est)


def per_device(
    core_fock,
    intersection,
    gamma_tile,
    charge_old,
    embed_old,
    core_pop,
    centres,
    frag_sizes,
    near_list,
    far_list,
):
    frag_dev = core_fock.shape[0]
    basis_count = core_fock.shape[2]
    tile_count = lax.axis_size("tile")
    tile_at = lax.axis_index("tile")
    frag_at = lax.axis_index("frag")
    column_index = jnp.arange(basis_count, dtype=jnp.int32)
    share_count = frag_dev // tile_count
    share_first = tile_at * share_count

    def select_share(array):
        return lax.dynamic_slice_in_dim(array, share_first, share_count, 0)

    stacked = jnp.stack([core_fock, intersection, gamma_tile], axis=1)
    whole_tiles = lax.all_to_all(stacked, "tile", split_axis=0, concat_axis=2, tiled=True)
    core_whole = whole_tiles[:, 0]
    over_whole = whole_tiles[:, 1]
    gamma_whole = whole_tiles[:, 2]
    field = jnp.einsum(
        "fij,fj->fi", gamma_whole, select_share(charge_old), precision=precise
    ) + select_share(embed_old)
    fock_matrix = core_whole + 0.5 * over_whole * (field[:, :, None] + field[:, None, :])
    density_whole = whole_density(fock_matrix, select_share(frag_sizes), column_index)
    charge_share = jnp.sum(density_whole * over_whole, axis=2) - select_share(core_pop)
    charges = lax.all_gather(charge_share, "tile", axis=0, tiled=True)
    table_own = jnp.concatenate([charges[:, None, :], centres], axis=1)
    blocks_own = point_blocks(charges, centres)
    far_table = lax.all_gather(blocks_own, "frag", axis=0, tiled=True)
    near_table = extended(table_own, (("frag", 0),), frag_dev)
    near_rows = near_list - (frag_at * frag_dev - frag_dev)
    potential = potentials(
        select_share(centres),
        select_share(near_rows),
        select_share(far_list),
        near_table,
        far_table,
    )
    esp_whole = 0.5 * over_whole * (potential[:, :, None] + potential[:, None, :])
    density, esp_matrix = (
        lax.all_to_all(density_whole, "tile", split_axis=1, concat_axis=0, tiled=True),
        lax.all_to_all(esp_whole, "tile", split_axis=1, concat_axis=0, tiled=True),
    )
    return (density, esp_matrix)


def solution(mesh):
    in_specs = (
        P("frag", "tile", None),
        P("frag", "tile", None),
        P("frag", "tile", None),
        P("frag", None),
        P("frag", None),
        P("frag", None),
        P("frag", None, None),
        P("frag"),
        P("frag", None),
        P("frag", None),
    )
    out_specs = (P("frag", "tile", None), P("frag", "tile", None))
    return jax.shard_map(
        per_device, mesh=mesh, in_specs=in_specs, out_specs=out_specs, check_vma=False
    )
```

profile of v0, /device:TPU:1, one launch (start us, length us, event | category | flops | bytes accessed | tf_op | source)
XLA Modules:
  0.0 191.0 jit_solution(5734987618957597006)
XLA Ops:
  0.6 2.7 %pad_maximum_fusion = f32[8,3,64,256]{3,2,1,0:T(8,128)} fusion(f32[8,1,64,256]{3,2,1,0:T(8,128)} %bitcast.134, f32[8,1,64,256]{3,2,1,0:T(8,128)} %bitcast.135, f32[8,1,64,256]{3,2,1,0:T(8,128)} %bitcast.136), kind=kLoop, calls=%fused_computation.26 | loop fusion | flops 786432 | bytes 3145728 | tf_op jit(solution)/shard_map/stack | solution.py:102
  3.3 5.0 %all-to-all-start = ((f32[8,3,64,256]{3,2,1,0:T(8,128)}), f32[8,3,64,256]{3,2,1,0:T(8,128)S(1)}, u32[]{:S(2)}, u32[]{:S(2)}) async-start(f32[8,3,64,256]{3,2,1,0:T(8,128)} %pad_maximum_fusion), calls=%async_computation | async-start | bytes 3145728 | tf_op jit(solution)/shard_map/all_to_all | solution.py:103
  8.6 0.8 copy.70
  10.3 1.3 constant_dynamic-slice_fusion.9
  12.2 15.0 %all-to-all-done = f32[8,3,64,256]{3,2,1,0:T(8,128)S(1)} async-done(((f32[8,3,64,256]{3,2,1,0:T(8,128)}), f32[8,3,64,256]{3,2,1,0:T(8,128)S(1)}, u32[]{:S(2)}, u32[]{:S(2)}) %all-to-all-start) | async-done | bytes 1572896 | tf_op jit(solution)/shard_map/all_to_all | solution.py:103
  27.2 1.2 copy.68
  29.2 0.7 bitcast_add_fusion
  30.1 1.1 multiply_reduce_fusion.3
  31.7 17.1 %while.31 = (s32[]{:T(128)}, f32[2,256,256]{2,1,0:T(8,128)S(1)}, s32[]{:T(128)}) while((s32[]{:T(128)}, f32[2,256,256]{2,1,0:T(8,128)S(1)}, s32[]{:T(128)}) %tuple.84), condition=%wide.region_2.0_spmd, body=%wide.region_1.0_spmd.sunk | while | flops 805699584 | bytes 3670061 | solution.py:74
  31.7 0.7 fusion.34
  32.4 0.7 fusion.35
  33.1 0.7 fusion.34
  33.8 0.7 fusion.35
  34.6 0.7 fusion.34
  35.2 0.7 fusion.35
  36.0 0.7 fusion.34
  36.7 0.7 fusion.35
  37.4 0.7 fusion.34
  38.1 0.7 fusion.35
  38.9 0.7 fusion.34
  39.5 0.7 fusion.35
  40.3 0.7 fusion.34
  41.0 0.7 fusion.35
  41.7 0.7 fusion.34
  42.4 0.7 fusion.35
  43.1 0.7 fusion.34
  43.8 0.7 fusion.35
  44.6 0.7 fusion.34
  45.2 0.7 fusion.35
  46.0 0.7 fusion.34
  46.7 0.7 fusion.35
  47.4 0.7 fusion.34
  48.1 0.7 fusion.35
  48.8 1.5 multiply_reduce_fusion.2
  50.6 8.1 %all-gather = f32[4,2,256]{2,1,0:T(2,128)S(1)} all-gather(f32[1,2,256]{2,1,0:T(2,128)S(1)} %copy.77), channel_id=1, replica_groups=mesh['frag'=64,'tile'=4] {'tile'}, dimensions={0}, use_global_device_ids=true | all-gather | bytes 10240 | tf_op jit(solution)/shard_map/all_gather | solution.py:113
  58.9 8.1 %collective-permute-start = (f32[8,4,256]{2,1,0:T(4,128)S(1)}, f32[8,4,256]{2,1,0:T(4,128)S(1)}, u32[]{:S(2)}, u32[]{:S(2)}) collective-permute-start(f32[8,4,256]{2,1,0:T(4,128)S(1)} %pad_maximum_fusion.2), channel_id=1, source_target_pairs={{0,4},{4,8},{8,12},{12,16},{16,20},{20,24},{24,28},{28,32},{32,36}... | collective-permute-start | bytes 98312 | tf_op jit(solution)/shard_map/ppermute | solution.py:21
  67.0 1.9 %collective-permute-start.1 = (f32[8,4,256]{2,1,0:T(4,128)S(1)}, f32[8,4,256]{2,1,0:T(4,128)S(1)}, u32[]{:S(2)}, u32[]{:S(2)}) collective-permute-start(f32[8,4,256]{2,1,0:T(4,128)S(1)} %pad_maximum_fusion.2), channel_id=1, source_target_pairs={{4,0},{8,4},{12,8},{16,12},{20,16},{24,20},{28,24},{32,28},{36,32}... | collective-permute-start | bytes 98312 | tf_op jit(solution)/shard_map/ppermute | solution.py:22
  69.1 3.5 %all-to-all-start.1 = ((f32[2,256,256]{2,0,1:T(2,128)}), f32[2,256,256]{2,0,1:T(2,128)S(1)}, u32[]{:S(2)}, u32[]{:S(2)}) async-start(f32[2,256,256]{2,0,1:T(2,128)} %get-tuple-element.139), calls=%async_computation.1 | async-start | bytes 1048576 | tf_op jit(solution)/shard_map/all_to_all | solution.py:128
  72.6 55.7 %all_gather.7 = f32[512,4,8]{2,1,0:T(4,128)S(1)} all-gather(f32[8,4,8]{2,1,0:T(4,128)S(1)} %copy.80), channel_id=1, replica_groups=mesh['frag'=64,'tile'=4] {'frag'}, dimensions={0}, use_global_device_ids=true | all-gather | bytes 66560 | tf_op jit(solution)/shard_map/all_gather | solution.py:116
  128.4 46.9 %while.33 = (s32[]{:T(128)}, f32[2,256]{1,0:T(2,128)S(1)}, s32[2,8]{1,0:T(2,128)S(1)}, f32[2,3,256]{2,1,0:T(4,128)S(1)}, f32[24,4,256]{2,1,0:T(4,128)S(1)}, /*in...) while((s32[]{:T(128)}, f32[2,256]{1,0:T(2,128)S(1)}, ...), condition=%wide.region_11.12_spmd, body=%wide.region_6.11_spmd.sunk | while | flops 902693 | bytes 59082 | solution.py:55
  129.5 22.2 %while.34 = (s32[]{:T(128)}, f32[256]{0:T(256)S(1)}, s32[8]{0:T(128)S(1)}, f32[24,4,256]{2,1,0:T(4,128)S(1)}, f32[3,256]{1,0:T(4,128)S(1)}, /*index=5*/s32[]{:T(...) while((s32[]{:T(128)}, f32[256]{0:T(256)S(1)}, s32[8]{0:T(128)S(1)}, ...), condition=%wide.region_9.9_spmd.clone, body=%wide.region_7.8_spmd.clone.sunk | while | flops 721161 | bytes 25817 | solution.py:51
  129.6 0.6 dynamic_slice.72
  153.0 22.2 %while.34 = (s32[]{:T(128)}, f32[256]{0:T(256)S(1)}, s32[8]{0:T(128)S(1)}, f32[24,4,256]{2,1,0:T(4,128)S(1)}, f32[3,256]{1,0:T(4,128)S(1)}, /*index=5*/s32[]{:T(...) while((s32[]{:T(128)}, f32[256]{0:T(256)S(1)}, s32[8]{0:T(128)S(1)}, ...), condition=%wide.region_9.9_spmd.clone, body=%wide.region_7.8_spmd.clone.sunk | while | flops 721161 | bytes 25817 | solution.py:51
  175.4 1.2 add_multiply_fusion.1
  176.5 4.5 %all-to-all-start.2 = ((f32[2,256,256]{2,0,1:T(2,128)}), f32[2,256,256]{2,0,1:T(2,128)S(1)}, u32[]{:S(2)}, u32[]{:S(2)}) async-start(f32[2,256,256]{2,0,1:T(2,128)} %add_multiply_fusion.1), calls=%async_computation.2 | async-start | bytes 1048576 | tf_op jit(solution)/shard_map/all_to_all | solution.py:129
  181.1 0.8 copy.74
  181.9 8.3 %all-to-all-done.2 = f32[2,256,256]{2,0,1:T(2,128)S(1)} async-done(((f32[2,256,256]{2,0,1:T(2,128)}), f32[2,256,256]{2,0,1:T(2,128)S(1)}, u32[]{:S(2)}, u32[]{:S(2)}) %all-to-all-start.2) | async-done | bytes 524320 | tf_op jit(solution)/shard_map/all_to_all | solution.py:129
  190.2 0.8 copy.82
  (182 shorter events, 20.4 us)
Async XLA Ops:
  0.6 9.1 %copy-start = (f32[8,256]{1,0:T(8,128)S(1)}, f32[8,256]{1,0:T(8,128)}, u32[]{:S(2)}) copy-start(f32[8,256]{1,0:T(8,128)} %param.19) | copy-start | bytes 24580
  3.3 5.0 %copy-start.13 = (s32[8]{0:T(128)S(1)}, s32[8]{0:T(128)}, u32[]{:S(2)}) copy-start(s32[8]{0:T(128)} %param.23) | copy-start | bytes 100
  3.3 5.1 %copy-start.4 = (f32[8,3,256]{2,0,1:T(8,128)S(1)}, f32[8,3,256]{2,0,1:T(8,128)}, u32[]{:S(2)}) copy-start(f32[8,3,256]{2,0,1:T(8,128)} %param.22) | copy-start | bytes 73732
  3.3 7.0 %copy-start.10 = (s32[8,8]{1,0:T(8,128)S(1)}, s32[8,8]{1,0:T(8,128)}, u32[]{:S(2)}) copy-start(s32[8,8]{1,0:T(8,128)} %param.24) | copy-start | bytes 772
  3.3 23.9 %all-to-all-start = ((f32[8,3,64,256]{3,2,1,0:T(8,128)}), f32[8,3,64,256]{3,2,1,0:T(8,128)S(1)}, u32[]{:S(2)}, u32[]{:S(2)}) async-start(f32[8,3,64,256]{3,2,1,0:T(8,128)} %pad_maximum_fusion), calls=%async_computation | async-start | bytes 3145728 | tf_op jit(solution)/shard_map/all_to_all | solution.py:103
  8.4 18.8 %copy-start.6 = (f32[2,256]{1,0:T(2,128)}, f32[2,256]{1,0:T(2,128)S(1)}, u32[]{:S(2)}) copy-start(f32[2,256]{1,0:T(2,128)S(1)} %compare_convert_fusion) | copy-start | bytes 6148
  8.6 3.0 %copy-start.2 = (f32[8,3,256]{2,1,0:T(4,128)}, f32[8,3,256]{2,1,0:T(4,128)S(1)}, u32[]{:S(2)}) copy-start(f32[8,3,256]{2,1,0:T(4,128)S(1)} %copy.75) | copy-start | bytes 73732
  27.2 1.4 copy-start.9
  28.4 1.7 copy-start.1
  28.4 1.6 copy-start.7
  48.8 10.0 %copy-start.3 = (f32[8,3,256]{2,1,0:T(4,128)S(1)}, f32[8,3,256]{2,1,0:T(4,128)}, u32[]{:S(2)}) copy-start(f32[8,3,256]{2,1,0:T(4,128)} %copy-done.2) | copy-start | bytes 73732
  48.8 20.2 %copy-start.5 = (f32[8,3,8]{2,0,1:T(8,128)S(1)}, f32[8,3,8]{2,0,1:T(8,128)}, u32[]{:S(2)}) copy-start(f32[8,3,8]{2,0,1:T(8,128)} %broadcast_multiply_fusion) | copy-start | bytes 2308
  50.5 77.9 %copy-start.8 = (f32[2,256]{1,0:T(2,128)S(1)}, f32[2,256]{1,0:T(2,128)}, u32[]{:S(2)}) copy-start(f32[2,256]{1,0:T(2,128)} %custom-call.3) | copy-start | bytes 6148
  50.5 77.9 %copy-start.11 = (s32[2,8]{1,0:T(2,128)S(1)}, s32[2,8]{1,0:T(2,128)}, u32[]{:S(2)}) copy-start(s32[2,8]{1,0:T(2,128)} %get-tuple-element.331) | copy-start | bytes 196
  50.5 77.9 %copy-start.12 = (s32[2,8]{1,0:T(2,128)S(1)}, s32[2,8]{1,0:T(2,128)}, u32[]{:S(2)}) copy-start(s32[2,8]{1,0:T(2,128)} %get-tuple-element.328) | copy-start | bytes 196
  58.9 69.4 %collective-permute-start = (f32[8,4,256]{2,1,0:T(4,128)S(1)}, f32[8,4,256]{2,1,0:T(4,128)S(1)}, u32[]{:S(2)}, u32[]{:S(2)}) collective-permute-start(f32[8,4,256]{2,1,0:T(4,128)S(1)} %pad_maximum_fusion.2), channel_id=1, source_target_pairs={{0,4},{4,8},{8,12},{12,16},{16,20},{20,24},{24,28},{28,32},{32,36}... | collective-permute-start | bytes 98312 | tf_op jit(solution)/shard_map/ppermute | solution.py:21
  67.0 61.2 %collective-permute-start.1 = (f32[8,4,256]{2,1,0:T(4,128)S(1)}, f32[8,4,256]{2,1,0:T(4,128)S(1)}, u32[]{:S(2)}, u32[]{:S(2)}) collective-permute-start(f32[8,4,256]{2,1,0:T(4,128)S(1)} %pad_maximum_fusion.2), channel_id=1, source_target_pairs={{4,0},{8,4},{12,8},{16,12},{20,16},{24,20},{28,24},{32,28},{36,32}... | collective-permute-start | bytes 98312 | tf_op jit(solution)/shard_map/ppermute | solution.py:22
  69.1 107.4 %all-to-all-start.1 = ((f32[2,256,256]{2,0,1:T(2,128)}), f32[2,256,256]{2,0,1:T(2,128)S(1)}, u32[]{:S(2)}, u32[]{:S(2)}) async-start(f32[2,256,256]{2,0,1:T(2,128)} %get-tuple-element.139), calls=%async_computation.1 | async-start | bytes 1048576 | tf_op jit(solution)/shard_map/all_to_all | solution.py:128
  176.5 13.7 %all-to-all-start.2 = ((f32[2,256,256]{2,0,1:T(2,128)}), f32[2,256,256]{2,0,1:T(2,128)S(1)}, u32[]{:S(2)}, u32[]{:S(2)}) async-start(f32[2,256,256]{2,0,1:T(2,128)} %add_multiply_fusion.1), calls=%async_computation.2 | async-start | bytes 1048576 | tf_op jit(solution)/shard_map/all_to_all | solution.py:129
where the time goes:
time: 192 us; the launch traced here: 191 us
  blocking collectives  63.8 us (33%)
  loops' own time  30.5 us (16%)
  waiting for transfers between devices  23.3 us (12%)
  starting transfers between devices  23 us (12%)
  local copies, waits for them, and re-layouts  19.4 us (10%)
  matrix products  16.8 us (9%)
  other arithmetic  13.2 us (7%)
    all_gather x1, blocking collectives, per_device(): far_table = lax.all_gather(blocks_own, 'frag', axis=0, tiled=True)  55.7 us
    another operation x2, loops' own time, potential_of(): lax.scan(add_near, jnp.zeros((basis_count,), jnp.float32), near_ids)  29.8 us
    all_to_all x1, waiting for transfers between devices, per_device(): lax.all_to_all(stacked, 'tile', split_axis=0, concat_axis=2, tiled=True)  15 us
    dynamic_slice x16, local copies, waits for them, and re-layouts, potential_of(): lax.scan(add_near, jnp.zeros((basis_count,), jnp.float32), near_ids)  9.87 us
    dot_general x12, matrix products, cube_step(): jnp.einsum('fij,fjk->fik', squared, full_rows, precision=precise)  8.36 us
    all_to_all x1, waiting for transfers between devices, per_device(): lax.all_to_all(esp_whole, 'tile', split_axis=1, concat_axis=0, tiled=True)  8.3 us
    ppermute x1, starting transfers between devices, extended(): before = lax.ppermute(last, axis, up)  8.15 us
    all_gather x1, blocking collectives, per_device(): charges = lax.all_gather(charge_share, 'tile', axis=0, tiled=True)  8.14 us
  transfers between devices with their start and end apart: 5, of which 2 were waited for; matrix products, arithmetic and copies ran while one was open for 12% of the time, Pallas kernels for 0%

commit v1 on v0

v1 whole, which is shorter than its diff:
```python
import functools
import jax
import jax.numpy as jnp
from jax import lax
from jax.experimental import pallas as pl
from jax.experimental.pallas import tpu as pltpu
from jax.sharding import PartitionSpec as P

ITERS = 12
TILES = 4
ROWS = 64
BASIS = 256
PER = 8
OWN = 2
PC = 8
LIST = 8
PLANES = 8

f32 = jnp.float32
bf16 = jnp.bfloat16
HI = lax.Precision.HIGHEST
MESH = pl.DeviceIdType.MESH


def dot_nt(a, b):
    return lax.dot_general(a, b, (((1,), (1,)), ((), ())), precision=HI, preferred_element_type=f32)


def split(x):
    high = x.astype(bf16)
    return high, (x - high.astype(f32)).astype(bf16)


def dot3(a, b):
    (ah, al), (bh, bl) = a, b
    mul = functools.partial(jnp.dot, preferred_element_type=f32)
    return mul(ah, bh) + mul(ah, bl) + mul(al, bh)


def lanes(shape):
    return lax.broadcasted_iota(jnp.int32, shape, len(shape) - 1)


def turn(x):
    return pltpu.roll(x, ROWS, axis=1)


def kernel(
    planes,
    groups,
    core_hbm,
    over_hbm,
    gamma_hbm,
    charge_hbm,
    embed_hbm,
    pop_hbm,
    centre_hbm,
    size_sm,
    near_sm,
    far_hbm,
    density_out,
    esp_out,
    core_v,
    over_v,
    gamma_v,
    charge_v,
    embed_v,
    pop_v,
    far_v,
    core_r,
    over_r,
    send1,
    send2,
    send3,
    got1,
    got2,
    got3,
    field_s,
    field_g,
    near_c,
    all_c,
    place_t,
    col_b,
    kern_n,
    kern_f,
    est,
    over_f,
    dens_s,
    table,
    block_t,
    col_s,
    in_sem,
    raw_send,
    raw_recv,
    fld_send,
    fld_recv,
    nc_send,
    nc_recv,
    ac_send,
    ac_recv,
    pl_send,
    pl_recv,
    tb_send,
    tb_recv,
    bd_send,
    bd_recv,
    bk_send,
    bk_recv,
    dn_send,
    dn_recv,
    out_sem,
):
    plane_frags = groups * PER
    plane_peers = groups * TILES
    at_f = lax.axis_index("frag")
    at_t = lax.axis_index("tile")
    at_z = at_f // groups
    at_g = lax.rem(at_f, groups)
    at_p = at_g * TILES + at_t
    frag_devs = planes * groups

    def tile_peer(step):
        return (at_f, lax.rem(at_t + step, TILES))

    def frag_peer(step):
        return (lax.rem(at_f + frag_devs + step, frag_devs), at_t)

    def plane_peer(step):
        peer = lax.rem(at_p + step, plane_peers)
        return (at_z * groups + peer // TILES, lax.rem(peer, TILES))

    def group_peer(step):
        return (at_z * groups + lax.rem(at_g + step, groups), at_t)

    def z_peer(step):
        return (lax.rem(at_z + planes + step, planes) * groups + at_g, at_t)

    barrier = pltpu.get_barrier_semaphore()

    def greet(device):
        pl.semaphore_signal(barrier, inc=1, device_id=device, device_id_type=MESH)

    def greet_plane(step, carry):
        greet(plane_peer(step))
        return carry

    def greet_z(step, carry):
        greet(z_peer(step))
        return carry

    lax.fori_loop(1, plane_peers, greet_plane, 0)
    lax.fori_loop(1, planes, greet_z, 0)
    greet(frag_peer(1))
    greet(frag_peer(-1))

    loads = [
        pltpu.make_async_copy(src, dst, in_sem.at[n])
        for n, (src, dst) in enumerate(
            (
                (core_hbm, core_v),
                (over_hbm, over_v),
                (gamma_hbm, gamma_v),
                (charge_hbm, charge_v),
                (embed_hbm, embed_v),
                (pop_hbm, pop_v),
                (far_hbm, far_v),
                (centre_hbm, near_c.at[1]),
                (centre_hbm, all_c.at[at_g]),
            )
        )
    ]
    for load in loads:
        load.start()

    back = lax.rem(BASIS - ROWS * at_t, BASIS)
    forth = ROWS * at_t
    lane128 = lanes((ROWS, 128))
    low = lane128 < ROWS
    to_prev = lax.rem(at_t + 3, TILES)
    to_opp = lax.rem(at_t + 2, TILES)
    to_next = lax.rem(at_t + 1, TILES)
    for n, (array, turned) in enumerate(((core_v, core_r), (over_v, over_r))):
        loads[n].wait()
        for f in range(PER):
            turned[f] = pltpu.roll(array[f], back, axis=1)
        firsts, pairs = [], []
        for e in range(OWN):
            mine = turned[OWN * to_prev + e]
            send1[n, e] = turn(mine[:, :128])
            firsts.append(mine[:, 128:])
            mine = turned[OWN * to_next + e]
            send3[n, e] = jnp.where(low, turn(mine[:, 128:]), turn(mine[:, :128]))
            pairs.append(turned[OWN * to_opp + e][:, :128])
        send1[n, 2] = jnp.where(low, firsts[0], turn(firsts[1]))
        send2[n, 0] = jnp.where(low, pairs[0], turn(pairs[1]))

    pl.semaphore_wait(barrier, (plane_peers - 1) + (planes - 1) + 2)

    sends = []

    def push(src, dst, send_sem, recv_sem, device):
        copy = pltpu.make_async_remote_copy(
            src_ref=src,
            dst_ref=dst,
            send_sem=send_sem,
            recv_sem=recv_sem,
            device_id=device,
            device_id_type=MESH,
        )
        copy.start()
        sends.append(copy)
        return copy

    raw = [
        push(send2, got2, raw_send.at[1], raw_recv.at[1], tile_peer(2)),
        push(send1, got1, raw_send.at[0], raw_recv.at[0], tile_peer(3)),
        push(send3, got3, raw_send.at[2], raw_recv.at[2], tile_peer(1)),
    ]
    near = [
        push(centre_hbm, near_c.at[0], nc_send.at[0], nc_recv.at[0], frag_peer(1)),
        push(centre_hbm, near_c.at[2], nc_send.at[1], nc_recv.at[1], frag_peer(-1)),
    ]

    def spread_centres(step, carry):
        pltpu.make_async_remote_copy(
            src_ref=centre_hbm,
            dst_ref=all_c.at[at_g],
            send_sem=ac_send,
            recv_sem=ac_recv,
            device_id=group_peer(step),
            device_id_type=MESH,
        ).start()
        return carry

    lax.fori_loop(1, groups, spread_centres, 0)

    for n in (2, 3, 4):
        loads[n].wait()
    wide = (PER, PER * ROWS)
    prod = dot_nt(charge_v[...], gamma_v[...].reshape(PER * ROWS, BASIS))
    emb = pltpu.roll(embed_v[...], back, axis=1)[:, :128]
    emb = jnp.where(lanes((PER, 128)) < ROWS, emb, turn(emb))
    prod = prod + jnp.concatenate([emb] * 4, axis=1)
    same = lax.broadcasted_iota(jnp.int32, wide, 0) == lanes(wide) // ROWS
    fields = jnp.sum(jnp.where(same, prod, 0.0), axis=0, keepdims=True)
    for t in range(TILES):
        field_s[t] = fields[:, 128 * t : 128 * t + 128]
    fld = []
    for r in (2, 1, 3):
        dest = lax.rem(at_t + TILES - r, TILES)
        fld.append(
            push(field_s.at[dest], field_g.at[r], fld_send.at[r - 1], fld_recv.at[r - 1], (at_f, dest))
        )

    loads[7].wait()
    own = near_c[1].reshape(3 * PER, BASIS)
    cols = jnp.transpose(jnp.concatenate([own, jnp.zeros((128 - 3 * PER, BASIS), f32)], axis=0))
    for f in range(PER):
        for d in range(3):
            n = d * PER + f
            col_b[f, d] = jnp.broadcast_to(cols[:, n : n + 1], (BASIS, 128))
    for copy in near:
        copy.wait_recv()
    near_first = at_f * PER - PER

    def pair(n, carry):
        f = n // LIST
        other = jnp.clip(near_sm[f, lax.rem(n, LIST)] - near_first, 0, 3 * PER - 1)
        slot = other // PER
        row = other - slot * PER
        src = [near_c[slot, d, pl.ds(row, 1), :] for d in range(3)]
        for r in range(4):
            rows = slice(64 * r, 64 * r + 64)
            for h in range(2):
                cut = slice(128 * h, 128 * h + 128)
                dist = 1.0
                for d in range(3):
                    diff = col_b[f, d, rows, :] - src[d][:, cut]
                    dist = dist + diff * diff
                kern_n[n, rows, cut] = lax.rsqrt(dist)
        return carry

    lax.fori_loop(0, PER * LIST, pair, 0)

    loads[8].wait()
    pltpu.make_async_copy(
        all_c.at[pl.ds(0, groups - 1)], all_c.at[pl.ds(0, groups - 1)], ac_recv
    ).wait()
    runs = lax.broadcasted_iota(jnp.int32, (PC, BASIS), 0) == lanes((PC, BASIS)) // (BASIS // PC)
    sum_run = runs.astype(f32)
    mean_run = sum_run * (PC / BASIS)
    pad = jnp.zeros((PC, 128 - plane_frags), f32)
    for d in range(3):
        places = dot_nt(mean_run, all_c[:, d].reshape(plane_frags, BASIS))
        place_t[at_z, d] = jnp.concatenate([places, pad], axis=1)

    def spread_places(step, carry):
        pltpu.make_async_remote_copy(
            src_ref=place_t.at[at_z],
            dst_ref=place_t.at[at_z],
            send_sem=pl_send,
            recv_sem=pl_recv,
            device_id=z_peer(step),
            device_id_type=MESH,
        ).start()
        return carry

    lax.fori_loop(1, planes, spread_places, 0)

    fld_rows = [field_s[at_t]]
    for copy in fld:
        copy.wait_recv()
    for r in (1, 2, 3):
        fld_rows.append(field_g[r])
    for copy in raw:
        copy.wait_recv()
    full_lanes = lanes((1, BASIS))
    low1 = lanes((1, 128)) < ROWS
    zero = jnp.zeros((ROWS, 128), f32)

    def halves(n, turned, e):
        top = turned[OWN * at_t + e]
        top = jnp.where(lanes((ROWS, BASIS)) < ROWS, 0.5 * top, top)
        one = got1[n, e]
        tail = got1[n, 2]
        tail = turn(tail) if e == 0 else tail
        opp = got2[n, 0]
        opp = opp if e == 0 else turn(opp)
        last = got3[n, e]
        return jnp.concatenate(
            [
                top,
                jnp.concatenate([jnp.where(low, 0.0, 0.5 * one), jnp.where(low, one, tail)], axis=1),
                jnp.concatenate([zero, jnp.where(low, 0.5 * opp, 0.0)], axis=1),
                jnp.concatenate([zero, jnp.where(low, last, 0.5 * last)], axis=1),
            ],
            axis=0,
        )

    square = (BASIS, BASIS)
    row_at = lax.broadcasted_iota(jnp.int32, square, 0)
    col_at = lanes(square)
    eye = (row_at == col_at).astype(f32)
    for e in range(OWN):
        half = halves(1, over_r, e)
        over = half + jnp.transpose(half)
        over_f[e] = over
        if e == 0:
            field = [jnp.where(low1, fld_rows[0], turn(fld_rows[1])), jnp.where(low1, fld_rows[2], turn(fld_rows[3]))]
        else:
            field = [jnp.where(low1, turn(fld_rows[0]), fld_rows[1]), jnp.where(low1, turn(fld_rows[2]), fld_rows[3])]
        field = jnp.concatenate(field, axis=1)
        half = halves(0, core_r, e) + 0.5 * over * field
        fock = half + jnp.transpose(half)
        size = size_sm[OWN * at_t + e]
        row_in = lax.rem(row_at + ROWS * at_t, BASIS) < size
        col_in = lax.rem(col_at + ROWS * at_t, BASIS) < size
        fock = jnp.where(row_in & col_in, fock, 0.0)
        total = jnp.sum(jnp.sum(fock * fock, axis=0, keepdims=True), axis=1, keepdims=True)
        fock = fock / jnp.sqrt(total + 1e-06)
        est[e] = fock + jnp.where(row_in, 0.0, eye)

    def sweep(step, carry):
        parts = [split(est[e]) for e in range(OWN)]
        squares = [split(dot3(parts[e], parts[e])) for e in range(OWN)]
        for e in range(OWN):
            est[e] = 1.5 * est[e] - 0.5 * dot3(squares[e], parts[e])
        return carry

    lax.fori_loop(0, ITERS, sweep, 0)

    loads[5].wait()
    first = PER + at_g * PER + OWN * at_t
    for e in range(OWN):
        dens = 0.5 * (eye - est[e])
        charge = jnp.sum(dens * over_f[e], axis=0, keepdims=True)
        charge = pltpu.roll(jnp.broadcast_to(charge, (8, BASIS)), forth, axis=1)[0:1]
        charge = charge - pop_v[pl.ds(OWN * at_t + e, 1), :]
        table[first + e] = charge

    def spread_charges(step, carry):
        pltpu.make_async_remote_copy(
            src_ref=table.at[pl.ds(first, OWN)],
            dst_ref=table.at[pl.ds(first, OWN)],
            send_sem=tb_send,
            recv_sem=tb_recv,
            device_id=plane_peer(step),
            device_id_type=MESH,
        ).start()
        return carry

    lax.fori_loop(1, plane_peers, spread_charges, 0)

    for e in range(OWN):
        dens = pltpu.roll(0.5 * (eye - est[e]), forth, axis=1)
        for r in range(TILES):
            dens_s[r, e] = dens[ROWS * r : ROWS * r + ROWS]
    slot = density_out.at[pl.ds(OWN * at_t, OWN)]
    den = [push(dens_s.at[r], slot, dn_send.at[r - 1], dn_recv.at[r - 1], tile_peer(r)) for r in (2, 1, 3)]
    keep = pltpu.make_async_copy(dens_s.at[0], slot, out_sem.at[0])
    keep.start()

    loads[6].wait()
    far_list = far_v[...].astype(f32)
    diag = lax.broadcasted_iota(jnp.int32, (LIST, LIST), 0) == lanes((LIST, LIST))
    far_at = [
        jnp.sum(jnp.where(diag, jnp.broadcast_to(far_list[f : f + 1], (LIST, LIST)), 0.0), axis=1, keepdims=True)
        for f in range(PER)
    ]
    far_at = jnp.broadcast_to(jnp.concatenate(far_at, axis=0), (PER * LIST, 128))
    lane64 = lanes((PER * LIST, 128))
    picks = []
    for z in range(planes):
        entry = jnp.where(lane64 < plane_frags, lane64 + z * plane_frags, -1).astype(f32)
        picks.append((far_at == entry).astype(f32))
    pick = jnp.concatenate(picks, axis=1)
    pltpu.make_async_copy(
        place_t.at[pl.ds(0, planes - 1)], place_t.at[pl.ds(0, planes - 1)], pl_recv
    ).wait()
    far_place = [
        dot_nt(pick, jnp.concatenate([place_t[z, d] for z in range(planes)], axis=1)) for d in range(3)
    ]
    spots = [
        jnp.concatenate([jnp.broadcast_to(near_c[1, d, f : f + 1, :], (LIST, BASIS)) for f in range(PER)], axis=0)
        for d in range(3)
    ]
    for p in range(PC):
        dist = 1.0
        for d in range(3):
            diff = spots[d] - far_place[d][:, p : p + 1]
            dist = dist + diff * diff
        kern_f[p] = lax.rsqrt(dist)

    pltpu.make_async_copy(
        table.at[pl.ds(PER, plane_frags - OWN)], table.at[pl.ds(PER, plane_frags - OWN)], tb_recv
    ).wait()
    plane_charge = table[pl.ds(PER, plane_frags)].reshape(plane_frags, BASIS)
    block_t[at_z] = jnp.concatenate([dot_nt(sum_run, plane_charge), pad], axis=1)

    edge = [
        push(table.at[pl.ds(plane_frags, PER)], table.at[pl.ds(0, PER)], bd_send.at[0], bd_recv.at[0], z_peer(1)),
        push(table.at[pl.ds(PER, PER)], table.at[pl.ds(plane_frags + PER, PER)], bd_send.at[1], bd_recv.at[1], z_peer(-1)),
    ]

    def spread_blocks(step, carry):
        pltpu.make_async_remote_copy(
            src_ref=block_t.at[at_z],
            dst_ref=block_t.at[at_z],
            send_sem=bk_send,
            recv_sem=bk_recv,
            device_id=z_peer(step),
            device_id_type=MESH,
        ).start()
        return carry

    lax.fori_loop(1, planes, spread_blocks, 0)

    for copy in edge:
        copy.wait_recv()
    table_first = at_z * plane_frags - PER
    lane256 = lanes((BASIS, 128))
    near_cols = jnp.zeros((BASIS, 128), f32)

    def near_sum(f):
        acc = jnp.zeros((BASIS, 128), f32)
        for k in range(LIST):
            row = table[jnp.clip(near_sm[f, k] - table_first, 0, plane_frags + 2 * PER - 1)]
            acc = acc + kern_n[f * LIST + k, :, :128] * row[:, :128]
            acc = acc + kern_n[f * LIST + k, :, 128:] * row[:, 128:]
        return jnp.sum(acc, axis=1, keepdims=True)

    def near_step(f, cols):
        return jnp.where(lane256 == f, near_sum(f), cols)

    near_cols = lax.fori_loop(0, PER, near_step, near_cols)
    near_rows = jnp.transpose(near_cols)[:PER]

    pltpu.make_async_copy(
        block_t.at[pl.ds(0, planes - 1)], block_t.at[pl.ds(0, planes - 1)], bk_recv
    ).wait()
    far_charge = dot_nt(pick, jnp.concatenate([block_t[z] for z in range(planes)], axis=1))
    far_sum = jnp.zeros((PER * LIST, BASIS), f32)
    for p in range(PC):
        far_sum = far_sum + far_charge[:, p : p + 1] * kern_f[p]
    far_rows = jnp.sum(far_sum.reshape(PER, LIST, BASIS), axis=1)
    potential = 0.25 * (near_rows + far_rows)
    col_s[...] = jnp.transpose(jnp.concatenate([potential, jnp.zeros((128 - PER, BASIS), f32)], axis=0))
    mine = col_s[pl.ds(ROWS * at_t, ROWS), :]
    for f in range(PER):
        esp_out[f] = 0.5 * over_v[f] * (mine[:, f : f + 1] + potential[f : f + 1, :])

    for copy in den:
        copy.wait_recv()
    keep.wait()
    for copy in sends:
        copy.wait_send()
    for ref, count, sem in (
        (all_c, groups - 1, ac_send),
        (place_t, planes - 1, pl_send),
        (table, plane_frags - OWN, tb_send),
        (block_t, planes - 1, bk_send),
    ):
        pltpu.make_async_copy(ref.at[pl.ds(0, count)], ref.at[pl.ds(0, count)], sem).wait()


def per_device(
    planes,
    groups,
    core_fock,
    intersection,
    gamma_tile,
    charge_old,
    embed_old,
    core_pop,
    centres,
    frag_sizes,
    near_list,
    far_list,
):
    dma = pltpu.SemaphoreType.DMA
    anyspace = pl.BlockSpec(memory_space=pl.ANY)
    smem = pl.BlockSpec(memory_space=pltpu.SMEM)
    vmem = pl.BlockSpec(memory_space=pltpu.VMEM)
    own = (PER, ROWS, BASIS)
    pieces = (ROWS, 128)
    plane_frags = groups * PER
    return pl.pallas_call(
        functools.partial(kernel, planes, groups),
        out_shape=(jax.ShapeDtypeStruct(own, f32), jax.ShapeDtypeStruct(own, f32)),
        in_specs=[anyspace] * 7 + [smem, smem, anyspace],
        out_specs=(anyspace, vmem),
        scratch_shapes=[
            pltpu.VMEM(own, f32),
            pltpu.VMEM(own, f32),
            pltpu.VMEM(own, f32),
            pltpu.VMEM((PER, BASIS), f32),
            pltpu.VMEM((PER, BASIS), f32),
            pltpu.VMEM((PER, BASIS), f32),
            pltpu.VMEM((PER, LIST), jnp.int32),
            pltpu.VMEM(own, f32),
            pltpu.VMEM(own, f32),
            pltpu.VMEM((2, 3) + pieces, f32),
            pltpu.VMEM((2, 1) + pieces, f32),
            pltpu.VMEM((2, 2) + pieces, f32),
            pltpu.VMEM((2, 3) + pieces, f32),
            pltpu.VMEM((2, 1) + pieces, f32),
            pltpu.VMEM((2, 2) + pieces, f32),
            pltpu.VMEM((TILES, 1, 128), f32),
            pltpu.VMEM((TILES, 1, 128), f32),
            pltpu.VMEM((3, 3, PER, BASIS), f32),
            pltpu.VMEM((groups, 3, PER, BASIS), f32),
            pltpu.VMEM((planes, 3, PC, 128), f32),
            pltpu.VMEM((PER, 3, BASIS, 128), f32),
            pltpu.VMEM((PER * LIST, BASIS, BASIS), f32),
            pltpu.VMEM((PC, PER * LIST, BASIS), f32),
            pltpu.VMEM((OWN, BASIS, BASIS), f32),
            pltpu.VMEM((OWN, BASIS, BASIS), f32),
            pltpu.VMEM((TILES, OWN, ROWS, BASIS), f32),
            pltpu.VMEM((plane_frags + 2 * PER, 1, BASIS), f32),
            pltpu.VMEM((planes, PC, 128), f32),
            pltpu.VMEM((BASIS, 128), f32),
            dma((9,)),
            dma((3,)),
            dma((3,)),
            dma((3,)),
            dma((3,)),
            dma((2,)),
            dma((2,)),
            dma,
            dma,
            dma,
            dma,
            dma,
            dma,
            dma((2,)),
            dma((2,)),
            dma,
            dma,
            dma((3,)),
            dma((3,)),
            dma((1,)),
        ],
        compiler_params=pltpu.CompilerParams(
            collective_id=0, has_side_effects=True, vmem_limit_bytes=60 * 1024 * 1024
        ),
        name="scc_cycle",
    )(
        core_fock,
        intersection,
        gamma_tile,
        charge_old,
        embed_old,
        core_pop,
        jnp.transpose(centres, (1, 0, 2)),
        frag_sizes,
        near_list,
        far_list,
    )


def solution(mesh):
    groups = mesh.shape["frag"] // PLANES
    return build(mesh, PLANES, groups)


def build(mesh, planes, groups):
    in_specs = (
        P("frag", "tile", None),
        P("frag", "tile", None),
        P("frag", "tile", None),
        P("frag", None),
        P("frag", None),
        P("frag", None),
        P("frag", None, None),
        P("frag"),
        P("frag", None),
        P("frag", None),
    )
    out_specs = (P("frag", "tile", None), P("frag", "tile", None))
    return jax.shard_map(
        functools.partial(per_device, planes, groups),
        mesh=mesh,
        in_specs=in_specs,
        out_specs=out_specs,
        check_vma=False,
    )
```

time: 192 us -> 47.4 us (0.25)
  blocking collectives: 63.8 us -> 0 us
  Pallas kernels: 0 us -> 43.9 us
  loops' own time: 30.5 us -> 0 us
  waiting for transfers between devices: 23.3 us -> 0 us
  starting transfers between devices: 23 us -> 0 us
  matrix products: 16.8 us -> 0 us
  local copies, waits for them, and re-layouts: 19.4 us -> 2.72 us
  other arithmetic: 13.2 us -> 0 us
    all_gather x2 -> x0, blocking collectives: 63.8 us -> none  [the longest x1 55.7 us: per_device(): far_table = lax.all_gather(blocks_own, 'frag', axis=0, tiled=True)]
    pallas_call x0 -> x1, Pallas kernels: none -> 43.9 us  [per_device(): pl.pallas_call(functools.partial(kernel, planes, groups), out_shape=(jax....]
    another operation x4 -> x0, loops' own time: 30.5 us -> none  [the longest x2 29.8 us: potential_of(): lax.scan(add_near, jnp.zeros((basis_count,), jnp.float32), near_ids)]
    all_to_all x3 -> x0, waiting for transfers between devices: 23.3 us -> none  [the longest x1 15 us: per_device(): lax.all_to_all(stacked, 'tile', split_axis=0, concat_axis=2, tiled=True)]
    dot_general x25 -> x0, matrix products: 16.8 us -> none  [the longest x12 8.36 us: cube_step(): jnp.einsum('fij,fjk->fik', squared, full_rows, precision=precise)]
    all_to_all x3 -> x0, starting transfers between devices: 13 us -> none  [the longest x1 4.96 us: per_device(): lax.all_to_all(stacked, 'tile', split_axis=0, concat_axis=2, tiled=True)]
    dynamic_slice x20 -> x0, local copies, waits for them, and re-layouts: 11.8 us -> none  [the longest x16 9.87 us: potential_of(): lax.scan(add_near, jnp.zeros((basis_count,), jnp.float32), near_ids)]
    ppermute x2 -> x0, starting transfers between devices: 10.1 us -> none  [the longest x1 8.15 us: extended(): before = lax.ppermute(last, axis, up)]
  transfers between devices with their start and end apart: 5 -> 0, of which waited for: 2 -> 0; matrix products, arithmetic and copies ran while one was open for 12% -> 0% of each run, Pallas kernels for 0% -> 0%
where the time goes in v1:
time: 47.4 us; the launch traced here: 47.2 us
  Pallas kernels  43.9 us (93%)
  local copies, waits for them, and re-layouts  2.72 us (6%)
  between operations  0.65 us (1%)
    pallas_call x1, Pallas kernels, per_device(): pl.pallas_call(functools.partial(kernel, planes, groups), out_shape=(jax....  43.9 us
    unnamed x4, local copies, waits for them, and re-layouts  2.72 us

profile of v1, /device:TPU:1, one launch (start us, length us, event | category | flops | bytes accessed | tf_op | source)
XLA Modules:
  0.0 47.2 jit_solution(16734635449704982553)
XLA Ops:
  0.6 43.9 %scc_cycle.1 = (f32[8,64,256]{2,1,0:T(8,128)}, f32[8,64,256]{2,1,0:T(8,128)}) custom-call(f32[8,64,256]{2,1,0:T(8,128)} %core_hbm.1, f32[8,64,256]{2,1,0:T(8,128)} %over_hbm.1, f32[8,64,256]{2,1,0:T(8,128)} %gamma_hbm.1, f32[8,256]{1,0:T(8,128)} %charge_hbm.1, f32[8,256]{1,0:T(8,128)} %embed_hbm.1, f32[8,256]{1,0:T(8,128)} %pop_hbm.1, f32[3,8,256]{2,1,0:T(8,128)} %bitcast.1, ...), custom_call_target="tpu_custom_call" | custom-call | tf_op jit(solution)/shard_map/scc_cycle/pallas_call | solution.py:527
  44.5 0.0 copy-start
  44.5 1.9 %copy.14 = f32[8,64,256]{2,1,0:T(8,128)} copy(f32[8,64,256]{2,1,0:T(8,128)} %get-tuple-element.4) | data formatting | bytes 1048576
  46.5 0.0 copy-done
  46.5 0.8 %copy.15 = f32[8,64,256]{2,1,0:T(8,128)} copy(f32[8,64,256]{2,1,0:T(8,128)S(1)} %copy-done) | data formatting | bytes 1048576
Async XLA Ops:
  44.5 1.9 %copy-start = (f32[8,64,256]{2,1,0:T(8,128)S(1)}, f32[8,64,256]{2,1,0:T(8,128)}, u32[]{:S(2)}) copy-start(f32[8,64,256]{2,1,0:T(8,128)} %get-tuple-element.5) | copy-start | bytes 1572868

commit v2 on v1

--- a/solution.py
+++ b/solution.py
@@ -15,6 +15,8 @@
 PC = 8
 LIST = 8
 PLANES = 8
+FIRST_PAIRS = 34
+NEXT_PAIRS = 50
 
 f32 = jnp.float32
 bf16 = jnp.bfloat16
@@ -35,6 +37,17 @@
     (ah, al), (bh, bl) = a, b
     mul = functools.partial(jnp.dot, preferred_element_type=f32)
     return mul(ah, bh) + mul(ah, bl) + mul(al, bh)
+
+
+def pick_nt(sel, b):
+    high = b.astype(bf16)
+    rest = b - high.astype(f32)
+    middle = rest.astype(bf16)
+    least = (rest - middle.astype(f32)).astype(bf16)
+    mul = functools.partial(
+        lax.dot_general, dimension_numbers=(((1,), (1,)), ((), ())), preferred_element_type=f32
+    )
+    return mul(sel, high) + mul(sel, middle) + mul(sel, least)
 
 
 def lanes(shape):
@@ -116,7 +129,6 @@
     at_t = lax.axis_index("tile")
     at_z = at_f // groups
     at_g = lax.rem(at_f, groups)
-    at_p = at_g * TILES + at_t
     frag_devs = planes * groups
 
     def tile_peer(step):
@@ -125,33 +137,23 @@
     def frag_peer(step):
         return (lax.rem(at_f + frag_devs + step, frag_devs), at_t)
 
-    def plane_peer(step):
-        peer = lax.rem(at_p + step, plane_peers)
-        return (at_z * groups + peer // TILES, lax.rem(peer, TILES))
+    deep = groups // 2
+    ring = lambda n, size: min(n, size - n)
+    steps = [(dx, dy, dc) for dx in range(TILES) for dy in range(deep) for dc in range(2)][1:]
+    steps.sort(key=lambda s: (-ring(s[0], TILES) - ring(s[1], deep), -s[2]))
+    at_c = lax.rem(at_g, 2)
+    peer_x = [lax.rem(at_t + dx, TILES) for dx in range(TILES)]
+    peer_g = [
+        [at_z * groups + 2 * lax.rem(at_g // 2 + dy, deep) + (1 - at_c if dc else at_c) for dc in range(2)]
+        for dy in range(deep)
+    ]
+    plane_devices = [(peer_g[dy][dc], peer_x[dx]) for dx, dy, dc in steps]
 
     def group_peer(step):
         return (at_z * groups + lax.rem(at_g + step, groups), at_t)
 
     def z_peer(step):
         return (lax.rem(at_z + planes + step, planes) * groups + at_g, at_t)
-
-    barrier = pltpu.get_barrier_semaphore()
-
-    def greet(device):
-        pl.semaphore_signal(barrier, inc=1, device_id=device, device_id_type=MESH)
-
-    def greet_plane(step, carry):
-        greet(plane_peer(step))
-        return carry
-
-    def greet_z(step, carry):
-        greet(z_peer(step))
-        return carry
-
-    lax.fori_loop(1, plane_peers, greet_plane, 0)
-    lax.fori_loop(1, planes, greet_z, 0)
-    greet(frag_peer(1))
-    greet(frag_peer(-1))
 
     loads = [
         pltpu.make_async_copy(src, dst, in_sem.at[n])
@@ -171,6 +173,18 @@
     ]
     for load in loads:
         load.start()
+
+    barrier = pltpu.get_barrier_semaphore()
+
+    def greet(device):
+        pl.semaphore_signal(barrier, inc=1, device_id=device, device_id_type=MESH)
+
+    z_steps = sorted(range(1, planes), key=lambda n: -ring(n, planes))
+    z_devices = [z_peer(step) for step in z_steps]
+    for device in z_devices + plane_devices:
+        greet(device)
+    greet(frag_peer(1))
+    greet(frag_peer(-1))
 
     back = lax.rem(BASIS - ROWS * at_t, BASIS)
     forth = ROWS * at_t
@@ -280,18 +294,18 @@
                 kern_n[n, rows, cut] = lax.rsqrt(dist)
         return carry
 
-    lax.fori_loop(0, PER * LIST, pair, 0)
+    lax.fori_loop(0, FIRST_PAIRS, pair, 0)
 
     loads[8].wait()
     pltpu.make_async_copy(
         all_c.at[pl.ds(0, groups - 1)], all_c.at[pl.ds(0, groups - 1)], ac_recv
     ).wait()
     runs = lax.broadcasted_iota(jnp.int32, (PC, BASIS), 0) == lanes((PC, BASIS)) // (BASIS // PC)
-    sum_run = runs.astype(f32)
-    mean_run = sum_run * (PC / BASIS)
+    mean_run = (runs.astype(f32) * (PC / BASIS)).astype(bf16)
+    sum_run = runs.astype(f32).astype(bf16)
     pad = jnp.zeros((PC, 128 - plane_frags), f32)
     for d in range(3):
-        places = dot_nt(mean_run, all_c[:, d].reshape(plane_frags, BASIS))
+        places = pick_nt(mean_run, all_c[:, d].reshape(plane_frags, BASIS))
         place_t[at_z, d] = jnp.concatenate([places, pad], axis=1)
 
     def spread_places(step, carry):
@@ -378,18 +392,15 @@
         charge = charge - pop_v[pl.ds(OWN * at_t + e, 1), :]
         table[first + e] = charge
 
-    def spread_charges(step, carry):
+    for device in plane_devices:
         pltpu.make_async_remote_copy(
             src_ref=table.at[pl.ds(first, OWN)],
             dst_ref=table.at[pl.ds(first, OWN)],
             send_sem=tb_send,
             recv_sem=tb_recv,
-            device_id=plane_peer(step),
+            device_id=device,
             device_id_type=MESH,
         ).start()
-        return carry
-
-    lax.fori_loop(1, plane_peers, spread_charges, 0)
 
     for e in range(OWN):
         dens = pltpu.roll(0.5 * (eye - est[e]), forth, axis=1)
@@ -413,13 +424,13 @@
     for z in range(planes):
         entry = jnp.where(lane64 < plane_frags, lane64 + z * plane_frags, -1).astype(f32)
         picks.append((far_at == entry).astype(f32))
-    pick = jnp.concatenate(picks, axis=1)
+    pick = jnp.concatenate(picks, axis=1).astype(bf16)
     pltpu.make_async_copy(
         place_t.at[pl.ds(0, planes - 1)], place_t.at[pl.ds(0, planes - 1)], pl_recv
     ).wait()
-    far_place = [
-        dot_nt(pick, jnp.concatenate([place_t[z, d] for z in range(planes)], axis=1)) for d in range(3)
-    ]
+    far_place = pick_nt(
+        pick, jnp.concatenate([place_t[z].reshape(3 * PC, 128) for z in range(planes)], axis=1)
+    )
     spots = [
         jnp.concatenate([jnp.broadcast_to(near_c[1, d, f : f + 1, :], (LIST, BASIS)) for f in range(PER)], axis=0)
         for d in range(3)
@@ -427,33 +438,34 @@
     for p in range(PC):
         dist = 1.0
         for d in range(3):
-            diff = spots[d] - far_place[d][:, p : p + 1]
+            diff = spots[d] - far_place[:, d * PC + p : d * PC + p + 1]
             dist = dist + diff * diff
         kern_f[p] = lax.rsqrt(dist)
+
+    lax.fori_loop(FIRST_PAIRS, NEXT_PAIRS, pair, 0)
 
     pltpu.make_async_copy(
         table.at[pl.ds(PER, plane_frags - OWN)], table.at[pl.ds(PER, plane_frags - OWN)], tb_recv
     ).wait()
     plane_charge = table[pl.ds(PER, plane_frags)].reshape(plane_frags, BASIS)
-    block_t[at_z] = jnp.concatenate([dot_nt(sum_run, plane_charge), pad], axis=1)
-
-    edge = [
-        push(table.at[pl.ds(plane_frags, PER)], table.at[pl.ds(0, PER)], bd_send.at[0], bd_recv.at[0], z_peer(1)),
-        push(table.at[pl.ds(PER, PER)], table.at[pl.ds(plane_frags + PER, PER)], bd_send.at[1], bd_recv.at[1], z_peer(-1)),
-    ]
-
-    def spread_blocks(step, carry):
+    block_t[at_z] = jnp.concatenate([pick_nt(sum_run, plane_charge), pad], axis=1)
+
+    for device in z_devices:
         pltpu.make_async_remote_copy(
             src_ref=block_t.at[at_z],
             dst_ref=block_t.at[at_z],
             send_sem=bk_send,
             recv_sem=bk_recv,
-            device_id=z_peer(step),
+            device_id=device,
             device_id_type=MESH,
         ).start()
-        return carry
-
-    lax.fori_loop(1, planes, spread_blocks, 0)
+
+    edge = [
+        push(table.at[pl.ds(plane_frags, PER)], table.at[pl.ds(0, PER)], bd_send.at[0], bd_recv.at[0], z_peer(1)),
+        push(table.at[pl.ds(PER, PER)], table.at[pl.ds(plane_frags + PER, PER)], bd_send.at[1], bd_recv.at[1], z_peer(-1)),
+    ]
+
+    lax.fori_loop(NEXT_PAIRS, PER * LIST, pair, 0)
 
     for copy in edge:
         copy.wait_recv()
@@ -478,7 +490,7 @@
     pltpu.make_async_copy(
         block_t.at[pl.ds(0, planes - 1)], block_t.at[pl.ds(0, planes - 1)], bk_recv
     ).wait()
-    far_charge = dot_nt(pick, jnp.concatenate([block_t[z] for z in range(planes)], axis=1))
+    far_charge = pick_nt(pick, jnp.concatenate([block_t[z] for z in range(planes)], axis=1))
     far_sum = jnp.zeros((PER * LIST, BASIS), f32)
     for p in range(PC):
         far_sum = far_sum + far_charge[:, p : p + 1] * kern_f[p]
@@ -518,17 +530,17 @@
     far_list,
 ):
     dma = pltpu.SemaphoreType.DMA
-    anyspace = pl.BlockSpec(memory_space=pl.ANY)
     smem = pl.BlockSpec(memory_space=pltpu.SMEM)
+    hbm = pl.BlockSpec(memory_space=pltpu.HBM)
     vmem = pl.BlockSpec(memory_space=pltpu.VMEM)
     own = (PER, ROWS, BASIS)
     pieces = (ROWS, 128)
     plane_frags = groups * PER
     return pl.pallas_call(
         functools.partial(kernel, planes, groups),
-        out_shape=(jax.ShapeDtypeStruct(own, f32), jax.ShapeDtypeStruct(own, f32)),
-        in_specs=[anyspace] * 7 + [smem, smem, anyspace],
-        out_specs=(anyspace, vmem),
+        out_shape=(pltpu.VMEM(own, f32), pltpu.VMEM(own, f32)),
+        in_specs=[hbm] * 7 + [smem, smem, hbm],
+        out_specs=(vmem, vmem),
         scratch_shapes=[
             pltpu.VMEM(own, f32),
             pltpu.VMEM(own, f32),

time: 47.4 us -> 43 us (0.907)
  Pallas kernels: 43.9 us -> 40.6 us
  local copies, waits for them, and re-layouts: 2.72 us -> 1.59 us
    pallas_call x1, Pallas kernels: 43.9 us -> 40.6 us  [per_device(): pl.pallas_call(functools.partial(kernel, planes, groups), out_shape=(pltp...]
    unnamed x4 -> x2, local copies, waits for them, and re-layouts: 2.72 us -> 1.59 us
where the time goes in v2:
time: 43 us; the launch traced here: 42.9 us
  Pallas kernels  40.6 us (94%)
  local copies, waits for them, and re-layouts  1.59 us (4%)
  between operations  0.64 us (1%)
    pallas_call x1, Pallas kernels, per_device(): pl.pallas_call(functools.partial(kernel, planes, groups), out_shape=(pltp...  40.6 us
    unnamed x2, local copies, waits for them, and re-layouts  1.59 us

profile of v2, /device:TPU:1, one launch (start us, length us, event | category | flops | bytes accessed | tf_op | source)
XLA Modules:
  0.0 42.9 jit_solution(1994242850105123690)
XLA Ops:
  0.6 40.6 %scc_cycle.1 = (f32[8,64,256]{2,1,0:T(8,128)S(1)}, f32[8,64,256]{2,1,0:T(8,128)S(1)}) custom-call(f32[8,64,256]{2,1,0:T(8,128)} %core_hbm.1, f32[8,64,256]{2,1,0:T(8,128)} %over_hbm.1, f32[8,64,256]{2,1,0:T(8,128)} %gamma_hbm.1, f32[8,256]{1,0:T(8,128)} %charge_hbm.1, f32[8,256]{1,0:T(8,128)} %embed_hbm.1, f32[8,256]{1,0:T(8,128)} %pop_hbm.1, ...), custom_call_target="tpu_custom_call" | custom-call | tf_op jit(solution)/shard_map/scc_cycle/pallas_call | solution.py:539
  41.3 0.8 %copy.14 = f32[8,64,256]{2,1,0:T(8,128)} copy(f32[8,64,256]{2,1,0:T(8,128)S(1)} %get-tuple-element.2) | data formatting | bytes 1048576
  42.1 0.8 %copy.15 = f32[8,64,256]{2,1,0:T(8,128)} copy(f32[8,64,256]{2,1,0:T(8,128)S(1)} %get-tuple-element.3) | data formatting | bytes 1048576

commit v3 on v2

--- a/solution.py
+++ b/solution.py
@@ -15,8 +15,8 @@
 PC = 8
 LIST = 8
 PLANES = 8
-FIRST_PAIRS = 34
-NEXT_PAIRS = 50
+FIRST_PAIRS = 31
+NEXT_PAIRS = 52
 
 f32 = jnp.float32
 bf16 = jnp.bfloat16
@@ -122,9 +122,9 @@
     dn_send,
     dn_recv,
     out_sem,
+    ready,
 ):
     plane_frags = groups * PER
-    plane_peers = groups * TILES
     at_f = lax.axis_index("frag")
     at_t = lax.axis_index("tile")
     at_z = at_f // groups
@@ -176,15 +176,16 @@
 
     barrier = pltpu.get_barrier_semaphore()
 
-    def greet(device):
-        pl.semaphore_signal(barrier, inc=1, device_id=device, device_id_type=MESH)
+    def signal(sem, device):
+        pl.semaphore_signal(sem, inc=1, device_id=device, device_id_type=MESH)
 
     z_steps = sorted(range(1, planes), key=lambda n: -ring(n, planes))
     z_devices = [z_peer(step) for step in z_steps]
-    for device in z_devices + plane_devices:
-        greet(device)
-    greet(frag_peer(1))
-    greet(frag_peer(-1))
+    tile_devices = [tile_peer(step) for step in (2, 1, 3)]
+    first_devices = tile_devices + [frag_peer(1), frag_peer(-1), z_peer(1), z_peer(-1)]
+    first_devices += [group_peer(step) for step in range(1, groups)]
+    for device in first_devices:
+        signal(barrier, device)
 
     back = lax.rem(BASIS - ROWS * at_t, BASIS)
     forth = ROWS * at_t
@@ -208,7 +209,7 @@
         send1[n, 2] = jnp.where(low, firsts[0], turn(firsts[1]))
         send2[n, 0] = jnp.where(low, pairs[0], turn(pairs[1]))
 
-    pl.semaphore_wait(barrier, (plane_peers - 1) + (planes - 1) + 2)
+    pl.semaphore_wait(barrier, len(first_devices))
 
     sends = []
 
@@ -230,14 +231,15 @@
         push(send1, got1, raw_send.at[0], raw_recv.at[0], tile_peer(3)),
         push(send3, got3, raw_send.at[2], raw_recv.at[2], tile_peer(1)),
     ]
+    loads[7].wait()
     near = [
-        push(centre_hbm, near_c.at[0], nc_send.at[0], nc_recv.at[0], frag_peer(1)),
-        push(centre_hbm, near_c.at[2], nc_send.at[1], nc_recv.at[1], frag_peer(-1)),
+        push(near_c.at[1], near_c.at[0], nc_send.at[0], nc_recv.at[0], frag_peer(1)),
+        push(near_c.at[1], near_c.at[2], nc_send.at[1], nc_recv.at[1], frag_peer(-1)),
     ]
 
     def spread_centres(step, carry):
         pltpu.make_async_remote_copy(
-            src_ref=centre_hbm,
+            src_ref=near_c.at[1],
             dst_ref=all_c.at[at_g],
             send_sem=ac_send,
             recv_sem=ac_recv,
@@ -247,6 +249,10 @@
         return carry
 
     lax.fori_loop(1, groups, spread_centres, 0)
+    for device in tile_devices:
+        signal(ready.at[0], device)
+    for step in (1, -1):
+        signal(ready.at[1], z_peer(step))
 
     for n in (2, 3, 4):
         loads[n].wait()
@@ -266,7 +272,6 @@
             push(field_s.at[dest], field_g.at[r], fld_send.at[r - 1], fld_recv.at[r - 1], (at_f, dest))
         )
 
-    loads[7].wait()
     own = near_c[1].reshape(3 * PER, BASIS)
     cols = jnp.transpose(jnp.concatenate([own, jnp.zeros((128 - 3 * PER, BASIS), f32)], axis=0))
     for f in range(PER):
@@ -275,6 +280,10 @@
             col_b[f, d] = jnp.broadcast_to(cols[:, n : n + 1], (BASIS, 128))
     for copy in near:
         copy.wait_recv()
+    pl.semaphore_wait(ready.at[1], 2)
+    for step in (2, -2):
+        signal(ready.at[2], z_peer(step))
+
     near_first = at_f * PER - PER
 
     def pair(n, carry):
@@ -307,19 +316,6 @@
     for d in range(3):
         places = pick_nt(mean_run, all_c[:, d].reshape(plane_frags, BASIS))
         place_t[at_z, d] = jnp.concatenate([places, pad], axis=1)
-
-    def spread_places(step, carry):
-        pltpu.make_async_remote_copy(
-            src_ref=place_t.at[at_z],
-            dst_ref=place_t.at[at_z],
-            send_sem=pl_send,
-            recv_sem=pl_recv,
-            device_id=z_peer(step),
-            device_id_type=MESH,
-        ).start()
-        return carry
-
-    lax.fori_loop(1, planes, spread_places, 0)
 
     fld_rows = [field_s[at_t]]
     for copy in fld:
@@ -381,6 +377,21 @@
             est[e] = 1.5 * est[e] - 0.5 * dot3(squares[e], parts[e])
         return carry
 
+    pl.semaphore_wait(ready.at[2], 2)
+
+    def spread_places(step, carry):
+        pltpu.make_async_remote_copy(
+            src_ref=place_t.at[at_z],
+            dst_ref=place_t.at[at_z],
+            send_sem=pl_send,
+            recv_sem=pl_recv,
+            device_id=z_peer(step),
+            device_id_type=MESH,
+        ).start()
+        return carry
+
+    lax.fori_loop(1, planes, spread_places, 0)
+
     lax.fori_loop(0, ITERS, sweep, 0)
 
     loads[5].wait()
@@ -392,6 +403,7 @@
         charge = charge - pop_v[pl.ds(OWN * at_t + e, 1), :]
         table[first + e] = charge
 
+    pl.semaphore_wait(ready.at[0], len(tile_devices))
     for device in plane_devices:
         pltpu.make_async_remote_copy(
             src_ref=table.at[pl.ds(first, OWN)],
@@ -513,6 +525,17 @@
         (block_t, planes - 1, bk_send),
     ):
         pltpu.make_async_copy(ref.at[pl.ds(0, count)], ref.at[pl.ds(0, count)], sem).wait()
+
+
+def store(density, esp, density_out, esp_out, sem):
+    copies = [
+        pltpu.make_async_copy(src, dst, sem.at[n])
+        for n, (src, dst) in enumerate(((density, density_out), (esp, esp_out)))
+    ]
+    for copy in copies:
+        copy.start()
+    for copy in copies:
+        copy.wait()
 
 
 def per_device(
@@ -536,7 +559,7 @@
     own = (PER, ROWS, BASIS)
     pieces = (ROWS, 128)
     plane_frags = groups * PER
-    return pl.pallas_call(
+    held = pl.pallas_call(
         functools.partial(kernel, planes, groups),
         out_shape=(pltpu.VMEM(own, f32), pltpu.VMEM(own, f32)),
         in_specs=[hbm] * 7 + [smem, smem, hbm],
@@ -591,6 +614,7 @@
             dma((3,)),
             dma((3,)),
             dma((1,)),
+            pltpu.SemaphoreType.REGULAR((3,)),
         ],
         compiler_params=pltpu.CompilerParams(
             collective_id=0, has_side_effects=True, vmem_limit_bytes=60 * 1024 * 1024
@@ -608,6 +632,15 @@
         near_list,
         far_list,
     )
+    return pl.pallas_call(
+        store,
+        out_shape=(jax.ShapeDtypeStruct(own, f32), jax.ShapeDtypeStruct(own, f32)),
+        in_specs=[vmem, vmem],
+        out_specs=(pl.BlockSpec(memory_space=pl.ANY), pl.BlockSpec(memory_space=pl.ANY)),
+        scratch_shapes=[dma((2,))],
+        compiler_params=pltpu.CompilerParams(vmem_limit_bytes=1024 * 1024),
+        name="store",
+    )(*held)
 
 
 def solution(mesh):

time: 43 us -> 40.6 us (0.944)
  local copies, waits for them, and re-layouts: 1.59 us -> 0 us
  Pallas kernels: 40.6 us -> 39.5 us
    pallas_call x1, Pallas kernels: 40.6 us -> 38.5 us  [per_device(): pl.pallas_call(functools.partial(kernel, planes, groups), out_shape=(pltp...]
    unnamed x2 -> x0, local copies, waits for them, and re-layouts: 1.59 us -> none
    pallas_call x0 -> x1, Pallas kernels: none -> 0.99 us  [per_device(): pl.pallas_call(store, out_shape=(jax.ShapeDtypeStruct(own, f32), jax.Shap...]
where the time goes in v3:
time: 40.6 us; the launch traced here: 40.1 us
  Pallas kernels  39.5 us (97%)
  between operations  0.64 us (2%)
    pallas_call x1, Pallas kernels, per_device(): pl.pallas_call(functools.partial(kernel, planes, groups), out_shape=(pltp...  38.5 us
    pallas_call x1, Pallas kernels, per_device(): pl.pallas_call(store, out_shape=(jax.ShapeDtypeStruct(own, f32), jax.Shap...  0.99 us

profile of v3, /device:TPU:1, one launch (start us, length us, event | category | flops | bytes accessed | tf_op | source)
XLA Modules:
  0.0 40.1 jit_solution(5109369526058549772)
XLA Ops:
  0.6 38.5 %scc_cycle.1 = (f32[8,64,256]{2,1,0:T(8,128)S(1)}, f32[8,64,256]{2,1,0:T(8,128)S(1)}) custom-call(f32[8,64,256]{2,1,0:T(8,128)} %core_hbm.1, f32[8,64,256]{2,1,0:T(8,128)} %over_hbm.1, f32[8,64,256]{2,1,0:T(8,128)} %gamma_hbm.1, f32[8,256]{1,0:T(8,128)} %charge_hbm.1, f32[8,256]{1,0:T(8,128)} %embed_hbm.1, f32[8,256]{1,0:T(8,128)} %pop_hbm.1, ...), custom_call_target="tpu_custom_call" | custom-call | tf_op jit(solution)/shard_map/scc_cycle/pallas_call | solution.py:562
  39.1 1.0 %store.1 = (f32[8,64,256]{2,1,0:T(8,128)}, f32[8,64,256]{2,1,0:T(8,128)}) custom-call(f32[8,64,256]{2,1,0:T(8,128)S(1)} %get-tuple-element.4.density, f32[8,64,256]{2,1,0:T(8,128)S(1)} %get-tuple-element.5.esp), custom_call_target="tpu_custom_call" | custom-call | tf_op jit(solution)/shard_map/store/pallas_call | solution.py:635

commit v4 on v3

--- a/solution.py
+++ b/solution.py
@@ -370,11 +370,28 @@
         fock = fock / jnp.sqrt(total + 1e-06)
         est[e] = fock + jnp.where(row_in, 0.0, eye)
 
+    def near_product(a, b):
+        mul = functools.partial(jnp.dot, preferred_element_type=f32)
+        both = mul(jnp.concatenate(a, axis=0), b[0])
+        rows = a[0].shape[0]
+        return both[:rows] + both[rows:] + mul(a[0], b[1])
+
     def sweep(step, carry):
-        parts = [split(est[e]) for e in range(OWN)]
-        squares = [split(dot3(parts[e], parts[e])) for e in range(OWN)]
+        now = [est[e] for e in range(OWN)]
+        for _ in range(6):
+            parts = [split(x) for x in now]
+            cuts = [slice(r, r + 128) for r in range(0, BASIS, 128)]
+            squares = [
+                [split(near_product([p[cut] for p in part], part)) for cut in cuts] for part in parts
+            ]
+            now = [
+                jnp.concatenate(
+                    [1.5 * x[cut] - 0.5 * near_product(y, part) for cut, y in zip(cuts, square)], axis=0
+                )
+                for x, square, part in zip(now, squares, parts)
+            ]
         for e in range(OWN):
-            est[e] = 1.5 * est[e] - 0.5 * dot3(squares[e], parts[e])
+            est[e] = now[e]
         return carry
 
     pl.semaphore_wait(ready.at[2], 2)
@@ -392,7 +409,7 @@
 
     lax.fori_loop(1, planes, spread_places, 0)
 
-    lax.fori_loop(0, ITERS, sweep, 0)
+    lax.fori_loop(0, ITERS // 6, sweep, 0)
 
     loads[5].wait()
     first = PER + at_g * PER + OWN * at_t

time: 40.6 us -> 38.5 us (0.948)
  Pallas kernels: 39.5 us -> 37.3 us
    pallas_call x1, Pallas kernels: 38.5 us -> 36.4 us  [per_device(): pl.pallas_call(functools.partial(kernel, planes, groups), out_shape=(pltp...]
where the time goes in v4:
time: 38.5 us; the launch traced here: 38 us
  Pallas kernels  37.3 us (97%)
  between operations  0.64 us (2%)
    pallas_call x1, Pallas kernels, per_device(): pl.pallas_call(functools.partial(kernel, planes, groups), out_shape=(pltp...  36.4 us
    pallas_call x1, Pallas kernels, per_device(): pl.pallas_call(store, out_shape=(jax.ShapeDtypeStruct(own, f32), jax.Shap...  0.99 us

profile of v4, /device:TPU:1, one launch (start us, length us, event | category | flops | bytes accessed | tf_op | source)
XLA Modules:
  0.0 38.0 jit_solution(12989638465380977955)
XLA Ops:
  0.6 36.4 %scc_cycle.1 = (f32[8,64,256]{2,1,0:T(8,128)S(1)}, f32[8,64,256]{2,1,0:T(8,128)S(1)}) custom-call(f32[8,64,256]{2,1,0:T(8,128)} %core_hbm.1, f32[8,64,256]{2,1,0:T(8,128)} %over_hbm.1, f32[8,64,256]{2,1,0:T(8,128)} %gamma_hbm.1, f32[8,256]{1,0:T(8,128)} %charge_hbm.1, f32[8,256]{1,0:T(8,128)} %embed_hbm.1, f32[8,256]{1,0:T(8,128)} %pop_hbm.1, ...), custom_call_target="tpu_custom_call" | custom-call | tf_op jit(solution)/shard_map/scc_cycle/pallas_call | solution.py:579
  37.0 1.0 %store.1 = (f32[8,64,256]{2,1,0:T(8,128)}, f32[8,64,256]{2,1,0:T(8,128)}) custom-call(f32[8,64,256]{2,1,0:T(8,128)S(1)} %get-tuple-element.4.density, f32[8,64,256]{2,1,0:T(8,128)S(1)} %get-tuple-element.5.esp), custom_call_target="tpu_custom_call" | custom-call | tf_op jit(solution)/shard_map/store/pallas_call | solution.py:652

commit v5 on v4

--- a/solution.py
+++ b/solution.py
@@ -15,8 +15,7 @@
 PC = 8
 LIST = 8
 PLANES = 8
-FIRST_PAIRS = 31
-NEXT_PAIRS = 52
+FIRST_PAIRS = 34
 
 f32 = jnp.float32
 bf16 = jnp.bfloat16
@@ -421,6 +420,21 @@
         table[first + e] = charge
 
     pl.semaphore_wait(ready.at[0], len(tile_devices))
+    def to_next_plane(end, step, row):
+        @pl.when(at_g == end)
+        def _():
+            for t in range(TILES):
+                pltpu.make_async_remote_copy(
+                    src_ref=table.at[pl.ds(first, OWN)],
+                    dst_ref=table.at[pl.ds(row + OWN * at_t, OWN)],
+                    send_sem=bd_send.at[step],
+                    recv_sem=bd_recv.at[step],
+                    device_id=(frag_peer(1 if step == 0 else -1)[0], t),
+                    device_id_type=MESH,
+                ).start()
+
+    to_next_plane(groups - 1, 0, 0)
+    to_next_plane(0, 1, plane_frags + PER)
     for device in plane_devices:
         pltpu.make_async_remote_copy(
             src_ref=table.at[pl.ds(first, OWN)],
@@ -471,7 +485,7 @@
             dist = dist + diff * diff
         kern_f[p] = lax.rsqrt(dist)
 
-    lax.fori_loop(FIRST_PAIRS, NEXT_PAIRS, pair, 0)
+    lax.fori_loop(FIRST_PAIRS, PER * LIST, pair, 0)
 
     pltpu.make_async_copy(
         table.at[pl.ds(PER, plane_frags - OWN)], table.at[pl.ds(PER, plane_frags - OWN)], tb_recv
@@ -489,15 +503,17 @@
             device_id_type=MESH,
         ).start()
 
-    edge = [
-        push(table.at[pl.ds(plane_frags, PER)], table.at[pl.ds(0, PER)], bd_send.at[0], bd_recv.at[0], z_peer(1)),
-        push(table.at[pl.ds(PER, PER)], table.at[pl.ds(plane_frags + PER, PER)], bd_send.at[1], bd_recv.at[1], z_peer(-1)),
-    ]
-
-    lax.fori_loop(NEXT_PAIRS, PER * LIST, pair, 0)
-
-    for copy in edge:
-        copy.wait_recv()
+    below = table.at[pl.ds(0, PER)]
+    above = table.at[pl.ds(plane_frags + PER, PER)]
+
+    @pl.when(at_g == 0)
+    def _():
+        pltpu.make_async_copy(below, below, bd_recv.at[0]).wait()
+
+    @pl.when(at_g == groups - 1)
+    def _():
+        pltpu.make_async_copy(above, above, bd_recv.at[1]).wait()
+
     table_first = at_z * plane_frags - PER
     lane256 = lanes((BASIS, 128))
     near_cols = jnp.zeros((BASIS, 128), f32)
@@ -535,6 +551,12 @@
     keep.wait()
     for copy in sends:
         copy.wait_send()
+    for end, step in ((groups - 1, 0), (0, 1)):
+
+        @pl.when(at_g == end)
+        def _():
+            pltpu.make_async_copy(below, below, bd_send.at[step]).wait()
+
     for ref, count, sem in (
         (all_c, groups - 1, ac_send),
         (place_t, planes - 1, pl_send),

time: 38.5 us -> 37.5 us (0.974)
  Pallas kernels: 37.3 us -> 36.7 us
    pallas_call x1, Pallas kernels: 36.4 us -> 35.7 us  [per_device(): pl.pallas_call(functools.partial(kernel, planes, groups), out_shape=(pltp...]
where the time goes in v5:
time: 37.5 us; the launch traced here: 37.3 us
  Pallas kernels  36.7 us (98%)
  between operations  0.64 us (2%)
    pallas_call x1, Pallas kernels, per_device(): pl.pallas_call(functools.partial(kernel, planes, groups), out_shape=(pltp...  35.7 us
    pallas_call x1, Pallas kernels, per_device(): pl.pallas_call(store, out_shape=(jax.ShapeDtypeStruct(own, f32), jax.Shap...  0.99 us

profile of v5, /device:TPU:1, one launch (start us, length us, event | category | flops | bytes accessed | tf_op | source)
XLA Modules:
  0.0 37.3 jit_solution(3415190544519905585)
XLA Ops:
  0.6 35.7 %scc_cycle.1 = (f32[8,64,256]{2,1,0:T(8,128)S(1)}, f32[8,64,256]{2,1,0:T(8,128)S(1)}) custom-call(f32[8,64,256]{2,1,0:T(8,128)} %core_hbm.1, f32[8,64,256]{2,1,0:T(8,128)} %over_hbm.1, f32[8,64,256]{2,1,0:T(8,128)} %gamma_hbm.1, f32[8,256]{1,0:T(8,128)} %charge_hbm.1, f32[8,256]{1,0:T(8,128)} %embed_hbm.1, f32[8,256]{1,0:T(8,128)} %pop_hbm.1, ...), custom_call_target="tpu_custom_call" | custom-call | tf_op jit(solution)/shard_map/scc_cycle/pallas_call | solution.py:601
  36.4 1.0 %store.1 = (f32[8,64,256]{2,1,0:T(8,128)}, f32[8,64,256]{2,1,0:T(8,128)}) custom-call(f32[8,64,256]{2,1,0:T(8,128)S(1)} %get-tuple-element.4.density, f32[8,64,256]{2,1,0:T(8,128)S(1)} %get-tuple-element.5.esp), custom_call_target="tpu_custom_call" | custom-call | tf_op jit(solution)/shard_map/store/pallas_call | solution.py:674

commit v6 on v5

--- a/solution.py
+++ b/solution.py
@@ -15,7 +15,8 @@
 PC = 8
 LIST = 8
 PLANES = 8
-FIRST_PAIRS = 34
+FIRST_PAIRS = 28
+NEXT_PAIRS = 56
 
 f32 = jnp.float32
 bf16 = jnp.bfloat16
@@ -93,6 +94,7 @@
     all_c,
     place_t,
     col_b,
+    pick_v,
     kern_n,
     kern_f,
     est,
@@ -271,12 +273,33 @@
             push(field_s.at[dest], field_g.at[r], fld_send.at[r - 1], fld_recv.at[r - 1], (at_f, dest))
         )
 
-    own = near_c[1].reshape(3 * PER, BASIS)
-    cols = jnp.transpose(jnp.concatenate([own, jnp.zeros((128 - 3 * PER, BASIS), f32)], axis=0))
+    own = near_c[1]
+    length = own[0] * own[0] + own[1] * own[1] + own[2] * own[2] + 1.0
+    own = own.reshape(3 * PER, BASIS)
+    cols = jnp.transpose(
+        jnp.concatenate([own, length, jnp.zeros((128 - 4 * PER, BASIS), f32)], axis=0)
+    )
     for f in range(PER):
         for d in range(3):
             n = d * PER + f
             col_b[f, d] = jnp.broadcast_to(cols[:, n : n + 1], (BASIS, 128))
+        n = 3 * PER + f
+        col_b[f, 3] = jnp.broadcast_to(cols[:, n : n + 1], (BASIS, 128))
+    loads[6].wait()
+    far_list = far_v[...].astype(f32)
+    diag = lax.broadcasted_iota(jnp.int32, (LIST, LIST), 0) == lanes((LIST, LIST))
+    far_at = [
+        jnp.sum(jnp.where(diag, jnp.broadcast_to(far_list[f : f + 1], (LIST, LIST)), 0.0), axis=1, keepdims=True)
+        for f in range(PER)
+    ]
+    far_at = jnp.broadcast_to(jnp.concatenate(far_at, axis=0), (PER * LIST, 128))
+    lane64 = lanes((PER * LIST, 128))
+    picks = []
+    for z in range(planes):
+        entry = jnp.where(lane64 < plane_frags, lane64 + z * plane_frags, -1).astype(f32)
+        picks.append((far_at == entry).astype(f32))
+    pick_v[...] = jnp.concatenate(picks, axis=1).astype(bf16)
+
     for copy in near:
         copy.wait_recv()
     pl.semaphore_wait(ready.at[1], 2)
@@ -291,15 +314,17 @@
         slot = other // PER
         row = other - slot * PER
         src = [near_c[slot, d, pl.ds(row, 1), :] for d in range(3)]
+        src_length = src[0] * src[0] + src[1] * src[1] + src[2] * src[2]
+        src = [-2.0 * x for x in src]
         for r in range(4):
             rows = slice(64 * r, 64 * r + 64)
             for h in range(2):
                 cut = slice(128 * h, 128 * h + 128)
-                dist = 1.0
-                for d in range(3):
-                    diff = col_b[f, d, rows, :] - src[d][:, cut]
-                    dist = dist + diff * diff
-                kern_n[n, rows, cut] = lax.rsqrt(dist)
+                dist = col_b[f, 3, rows, :] + src_length[:, cut]
+                dot = col_b[f, 0, rows, :] * src[0][:, cut]
+                for d in (1, 2):
+                    dot = dot + col_b[f, d, rows, :] * src[d][:, cut]
+                kern_n[n, rows, cut] = lax.rsqrt(dist + dot)
         return carry
 
     lax.fori_loop(0, FIRST_PAIRS, pair, 0)
@@ -454,20 +479,7 @@
     keep = pltpu.make_async_copy(dens_s.at[0], slot, out_sem.at[0])
     keep.start()
 
-    loads[6].wait()
-    far_list = far_v[...].astype(f32)
-    diag = lax.broadcasted_iota(jnp.int32, (LIST, LIST), 0) == lanes((LIST, LIST))
-    far_at = [
-        jnp.sum(jnp.where(diag, jnp.broadcast_to(far_list[f : f + 1], (LIST, LIST)), 0.0), axis=1, keepdims=True)
-        for f in range(PER)
-    ]
-    far_at = jnp.broadcast_to(jnp.concatenate(far_at, axis=0), (PER * LIST, 128))
-    lane64 = lanes((PER * LIST, 128))
-    picks = []
-    for z in range(planes):
-        entry = jnp.where(lane64 < plane_frags, lane64 + z * plane_frags, -1).astype(f32)
-        picks.append((far_at == entry).astype(f32))
-    pick = jnp.concatenate(picks, axis=1).astype(bf16)
+    pick = pick_v[...]
     pltpu.make_async_copy(
         place_t.at[pl.ds(0, planes - 1)], place_t.at[pl.ds(0, planes - 1)], pl_recv
     ).wait()
@@ -485,7 +497,7 @@
             dist = dist + diff * diff
         kern_f[p] = lax.rsqrt(dist)
 
-    lax.fori_loop(FIRST_PAIRS, PER * LIST, pair, 0)
+    lax.fori_loop(FIRST_PAIRS, NEXT_PAIRS, pair, 0)
 
     pltpu.make_async_copy(
         table.at[pl.ds(PER, plane_frags - OWN)], table.at[pl.ds(PER, plane_frags - OWN)], tb_recv
@@ -502,6 +514,8 @@
             device_id=device,
             device_id_type=MESH,
         ).start()
+
+    lax.fori_loop(NEXT_PAIRS, PER * LIST, pair, 0)
 
     below = table.at[pl.ds(0, PER)]
     above = table.at[pl.ds(plane_frags + PER, PER)]
@@ -624,7 +638,8 @@
             pltpu.VMEM((3, 3, PER, BASIS), f32),
             pltpu.VMEM((groups, 3, PER, BASIS), f32),
             pltpu.VMEM((planes, 3, PC, 128), f32),
-            pltpu.VMEM((PER, 3, BASIS, 128), f32),
+            pltpu.VMEM((PER, 4, BASIS, 128), f32),
+            pltpu.VMEM((PER * LIST, planes * 128), bf16),
             pltpu.VMEM((PER * LIST, BASIS, BASIS), f32),
             pltpu.VMEM((PC, PER * LIST, BASIS), f32),
             pltpu.VMEM((OWN, BASIS, BASIS), f32),

time: 37.5 us -> 37.5 us (level)
  no operation moved by 1% of the time
where the time goes in v6:
time: 37.5 us; the launch traced here: 37.3 us
  Pallas kernels  36.7 us (98%)
  between operations  0.64 us (2%)
    pallas_call x1, Pallas kernels, per_device(): pl.pallas_call(functools.partial(kernel, planes, groups), out_shape=(pltp...  35.7 us
    pallas_call x1, Pallas kernels, per_device(): pl.pallas_call(store, out_shape=(jax.ShapeDtypeStruct(own, f32), jax.Shap...  0.99 us

profile of v6, /device:TPU:1, one launch (start us, length us, event | category | flops | bytes accessed | tf_op | source)
XLA Modules:
  0.0 37.3 jit_solution(6462711463065064230)
XLA Ops:
  0.6 35.7 %scc_cycle.1 = (f32[8,64,256]{2,1,0:T(8,128)S(1)}, f32[8,64,256]{2,1,0:T(8,128)S(1)}) custom-call(f32[8,64,256]{2,1,0:T(8,128)} %core_hbm.1, f32[8,64,256]{2,1,0:T(8,128)} %over_hbm.1, f32[8,64,256]{2,1,0:T(8,128)} %gamma_hbm.1, f32[8,256]{1,0:T(8,128)} %charge_hbm.1, f32[8,256]{1,0:T(8,128)} %embed_hbm.1, f32[8,256]{1,0:T(8,128)} %pop_hbm.1, ...), custom_call_target="tpu_custom_call" | custom-call | tf_op jit(solution)/shard_map/scc_cycle/pallas_call | solution.py:615
  36.3 1.0 %store.1 = (f32[8,64,256]{2,1,0:T(8,128)}, f32[8,64,256]{2,1,0:T(8,128)}) custom-call(f32[8,64,256]{2,1,0:T(8,128)S(1)} %get-tuple-element.4.density, f32[8,64,256]{2,1,0:T(8,128)S(1)} %get-tuple-element.5.esp), custom_call_target="tpu_custom_call" | custom-call | tf_op jit(solution)/shard_map/store/pallas_call | solution.py:689

commit v7 on v6

--- a/solution.py
+++ b/solution.py
@@ -15,8 +15,7 @@
 PC = 8
 LIST = 8
 PLANES = 8
-FIRST_PAIRS = 28
-NEXT_PAIRS = 56
+FIRST_PAIRS = 35
 
 f32 = jnp.float32
 bf16 = jnp.bfloat16
@@ -195,7 +194,22 @@
     to_prev = lax.rem(at_t + 3, TILES)
     to_opp = lax.rem(at_t + 2, TILES)
     to_next = lax.rem(at_t + 1, TILES)
-    for n, (array, turned) in enumerate(((core_v, core_r), (over_v, over_r))):
+    sends = []
+
+    def push(src, dst, send_sem, recv_sem, device):
+        copy = pltpu.make_async_remote_copy(
+            src_ref=src,
+            dst_ref=dst,
+            send_sem=send_sem,
+            recv_sem=recv_sem,
+            device_id=device,
+            device_id_type=MESH,
+        )
+        copy.start()
+        sends.append(copy)
+        return copy
+
+    def pack(n, array, turned):
         loads[n].wait()
         for f in range(PER):
             turned[f] = pltpu.roll(array[f], back, axis=1)
@@ -210,33 +224,26 @@
         send1[n, 2] = jnp.where(low, firsts[0], turn(firsts[1]))
         send2[n, 0] = jnp.where(low, pairs[0], turn(pairs[1]))
 
+    def send_packed(n):
+        return [
+            push(send2.at[n], got2.at[n], raw_send.at[n, 1], raw_recv.at[n, 1], tile_peer(2)),
+            push(send1.at[n], got1.at[n], raw_send.at[n, 0], raw_recv.at[n, 0], tile_peer(3)),
+            push(send3.at[n], got3.at[n], raw_send.at[n, 2], raw_recv.at[n, 2], tile_peer(1)),
+        ]
+
+    pack(0, core_v, core_r)
+
     pl.semaphore_wait(barrier, len(first_devices))
 
-    sends = []
-
-    def push(src, dst, send_sem, recv_sem, device):
-        copy = pltpu.make_async_remote_copy(
-            src_ref=src,
-            dst_ref=dst,
-            send_sem=send_sem,
-            recv_sem=recv_sem,
-            device_id=device,
-            device_id_type=MESH,
-        )
-        copy.start()
-        sends.append(copy)
-        return copy
-
-    raw = [
-        push(send2, got2, raw_send.at[1], raw_recv.at[1], tile_peer(2)),
-        push(send1, got1, raw_send.at[0], raw_recv.at[0], tile_peer(3)),
-        push(send3, got3, raw_send.at[2], raw_recv.at[2], tile_peer(1)),
-    ]
+    raw = send_packed(0)
     loads[7].wait()
     near = [
         push(near_c.at[1], near_c.at[0], nc_send.at[0], nc_recv.at[0], frag_peer(1)),
         push(near_c.at[1], near_c.at[2], nc_send.at[1], nc_recv.at[1], frag_peer(-1)),
     ]
+
+    pack(1, over_v, over_r)
+    raw += send_packed(1)
 
     def spread_centres(step, carry):
         pltpu.make_async_remote_copy(
@@ -497,7 +504,7 @@
             dist = dist + diff * diff
         kern_f[p] = lax.rsqrt(dist)
 
-    lax.fori_loop(FIRST_PAIRS, NEXT_PAIRS, pair, 0)
+    lax.fori_loop(FIRST_PAIRS, PER * LIST, pair, 0)
 
     pltpu.make_async_copy(
         table.at[pl.ds(PER, plane_frags - OWN)], table.at[pl.ds(PER, plane_frags - OWN)], tb_recv
@@ -514,8 +521,6 @@
             device_id=device,
             device_id_type=MESH,
         ).start()
-
-    lax.fori_loop(NEXT_PAIRS, PER * LIST, pair, 0)
 
     below = table.at[pl.ds(0, PER)]
     above = table.at[pl.ds(plane_frags + PER, PER)]
@@ -649,8 +654,8 @@
             pltpu.VMEM((planes, PC, 128), f32),
             pltpu.VMEM((BASIS, 128), f32),
             dma((9,)),
-            dma((3,)),
-            dma((3,)),
+            dma((2, 3)),
+            dma((2, 3)),
             dma((3,)),
             dma((3,)),
             dma((2,)),

time: 37.5 us -> 38.4 us (1.024)
  the two profiles are of different devices: /device:TPU:1 before, /device:TPU:32 now
where the time goes in v7:
time: 38.4 us; the launch traced here: 38.3 us
  Pallas kernels  37.6 us (98%)
  between operations  0.64 us (2%)
    pallas_call x1, Pallas kernels, per_device(): pl.pallas_call(functools.partial(kernel, planes, groups), out_shape=(pltp...  36.6 us
    pallas_call x1, Pallas kernels, per_device(): pl.pallas_call(store, out_shape=(jax.ShapeDtypeStruct(own, f32), jax.Shap...  0.99 us

profile of v7, /device:TPU:32, one launch (start us, length us, event | category | flops | bytes accessed | tf_op | source)
XLA Modules:
  0.0 38.3 jit_solution(18122268056490752389)
XLA Ops:
  0.6 36.6 %scc_cycle.1 = (f32[8,64,256]{2,1,0:T(8,128)S(1)}, f32[8,64,256]{2,1,0:T(8,128)S(1)}) custom-call(f32[8,64,256]{2,1,0:T(8,128)} %core_hbm.1, f32[8,64,256]{2,1,0:T(8,128)} %over_hbm.1, f32[8,64,256]{2,1,0:T(8,128)} %gamma_hbm.1, f32[8,256]{1,0:T(8,128)} %charge_hbm.1, f32[8,256]{1,0:T(8,128)} %embed_hbm.1, f32[8,256]{1,0:T(8,128)} %pop_hbm.1, ...), custom_call_target="tpu_custom_call" | custom-call | tf_op jit(solution)/shard_map/scc_cycle/pallas_call | solution.py:620
  37.3 1.0 %store.1 = (f32[8,64,256]{2,1,0:T(8,128)}, f32[8,64,256]{2,1,0:T(8,128)}) custom-call(f32[8,64,256]{2,1,0:T(8,128)S(1)} %get-tuple-element.4.density, f32[8,64,256]{2,1,0:T(8,128)S(1)} %get-tuple-element.5.esp), custom_call_target="tpu_custom_call" | custom-call | tf_op jit(solution)/shard_map/store/pallas_call | solution.py:694

commit v8 on v6

--- a/solution.py
+++ b/solution.py
@@ -15,8 +15,7 @@
 PC = 8
 LIST = 8
 PLANES = 8
-FIRST_PAIRS = 28
-NEXT_PAIRS = 56
+FIRST_PAIRS = 30
 
 f32 = jnp.float32
 bf16 = jnp.bfloat16
@@ -402,7 +401,7 @@
 
     def sweep(step, carry):
         now = [est[e] for e in range(OWN)]
-        for _ in range(6):
+        for _ in range(12):
             parts = [split(x) for x in now]
             cuts = [slice(r, r + 128) for r in range(0, BASIS, 128)]
             squares = [
@@ -433,7 +432,7 @@
 
     lax.fori_loop(1, planes, spread_places, 0)
 
-    lax.fori_loop(0, ITERS // 6, sweep, 0)
+    lax.fori_loop(0, ITERS // 12, sweep, 0)
 
     loads[5].wait()
     first = PER + at_g * PER + OWN * at_t
@@ -497,7 +496,7 @@
             dist = dist + diff * diff
         kern_f[p] = lax.rsqrt(dist)
 
-    lax.fori_loop(FIRST_PAIRS, NEXT_PAIRS, pair, 0)
+    lax.fori_loop(FIRST_PAIRS, PER * LIST, pair, 0)
 
     pltpu.make_async_copy(
         table.at[pl.ds(PER, plane_frags - OWN)], table.at[pl.ds(PER, plane_frags - OWN)], tb_recv
@@ -514,8 +513,6 @@
             device_id=device,
             device_id_type=MESH,
         ).start()
-
-    lax.fori_loop(NEXT_PAIRS, PER * LIST, pair, 0)
 
     below = table.at[pl.ds(0, PER)]
     above = table.at[pl.ds(plane_frags + PER, PER)]

time: 37.5 us -> 37.5 us (level)
  no operation moved by 1% of the time
where the time goes in v8:
time: 37.5 us; the launch traced here: 37.3 us
  Pallas kernels  36.6 us (98%)
  between operations  0.64 us (2%)
    pallas_call x1, Pallas kernels, per_device(): pl.pallas_call(functools.partial(kernel, planes, groups), out_shape=(pltp...  35.7 us
    pallas_call x1, Pallas kernels, per_device(): pl.pallas_call(store, out_shape=(jax.ShapeDtypeStruct(own, f32), jax.Shap...  0.99 us

profile of v8, /device:TPU:1, one launch (start us, length us, event | category | flops | bytes accessed | tf_op | source)
XLA Modules:
  0.0 37.3 jit_solution(11656829774095875956)
XLA Ops:
  0.6 35.7 %scc_cycle.1 = (f32[8,64,256]{2,1,0:T(8,128)S(1)}, f32[8,64,256]{2,1,0:T(8,128)S(1)}) custom-call(f32[8,64,256]{2,1,0:T(8,128)} %core_hbm.1, f32[8,64,256]{2,1,0:T(8,128)} %over_hbm.1, f32[8,64,256]{2,1,0:T(8,128)} %gamma_hbm.1, f32[8,256]{1,0:T(8,128)} %charge_hbm.1, f32[8,256]{1,0:T(8,128)} %embed_hbm.1, f32[8,256]{1,0:T(8,128)} %pop_hbm.1, ...), custom_call_target="tpu_custom_call" | custom-call | tf_op jit(solution)/shard_map/scc_cycle/pallas_call | solution.py:612
  36.3 1.0 %store.1 = (f32[8,64,256]{2,1,0:T(8,128)}, f32[8,64,256]{2,1,0:T(8,128)}) custom-call(f32[8,64,256]{2,1,0:T(8,128)S(1)} %get-tuple-element.4.density, f32[8,64,256]{2,1,0:T(8,128)S(1)} %get-tuple-element.5.esp), custom_call_target="tpu_custom_call" | custom-call | tf_op jit(solution)/shard_map/store/pallas_call | solution.py:686
